TPU v7x, 1024 devices: a whole 4x8x16 slice. The times are simulated.
1024 devices in a mesh: tm: 8 (over y_lo, core), height: 16 (over z), dp: 8 (over x, y_hi).
Axes of the slice: x: 4, y: 8 (y_hi: 2, y_lo: 4; y = y_hi * 4 + y_lo), z: 16, core: 2. Of those that a mesh axis runs over, the one named last changes fastest.
Arguments:
- queries: bfloat16 [8, 16, 16, 1, 192, 128], P('tm', 'height', 'dp'), may hold values from -4.5 to 4.5
- keys: bfloat16 [8, 16, 16, 1, 192, 128], P('tm', 'height', 'dp'), may hold values from -4.5 to 4.5
- values: bfloat16 [8, 16, 16, 1, 192, 128], P('tm', 'height', 'dp'), may hold values from -6 to 6
- grad_out: bfloat16 [8, 16, 16, 1, 192, 128], P('tm', 'height', 'dp'), may hold values from -24 to 24
- attn_out: bfloat16 [8, 16, 16, 1, 192, 128], P('tm', 'height', 'dp'), may hold values from -1.796875 to 1.796875
- window_mask: int32 [8, 16, 1, 27], P('tm', 'height'), may hold values 0 or 1
Outputs:
- grad_queries: bfloat16 [8, 16, 16, 1, 192, 128], P('tm', 'height', 'dp')
- grad_keys: bfloat16 [8, 16, 16, 1, 192, 128], P('tm', 'height', 'dp')
- grad_values: bfloat16 [8, 16, 16, 1, 192, 128], P('tm', 'height', 'dp')
All inputs are finite; a program needn't handle non-finite values. No bound on the sum of `window_mask` on one device may be relied on, other than what follows from the above.
Results may differ from a plain program's by a relative error of at most 0.009.
Values may be sent and summed in bfloat16 or wider, within the bound.
A program may use at most 32 MiB of HBM per device.

v0:
```python
import jax
import jax.numpy as jnp
from jax import lax
from jax.sharding import PartitionSpec as P


def with_halo(value, sides, width):
    for axis, dim in sides:
        size, length = (lax.axis_size(axis), value.shape[dim])
        up = [(i, (i + 1) % size) for i in range(size - 1)]
        down = [(j, i) for i, j in up]
        last = lax.slice_in_dim(value, length - width, length, axis=dim)
        initial = lax.slice_in_dim(value, 0, width, axis=dim)
        before = lax.ppermute(last, axis, up)
        after = lax.ppermute(initial, axis, down)
        value = jnp.concatenate([before, value, after], axis=dim)
    return value


def from_behind(block, axis, distance):
    devices = range(lax.axis_size(axis))
    route = [(i - distance, i) for i in devices if i - distance in devices]
    return lax.ppermute(block, axis, route)


def tile_scores(query_rows, key_rows, score_scale):
    return (
        jnp.einsum("hwqd,hwkd->hwqk", query_rows, key_rows, preferred_element_type=jnp.float32)
        * score_scale
    )


def probs_and_grads(
    query_rows, grad_rows, log_rows, delta_part, key_rows, value_rows, allowed, score_scale
):
    scores = tile_scores(query_rows, key_rows, score_scale)
    prob_weights = jnp.where(
        allowed[None, :, None, None], jnp.exp(scores - log_rows[..., None]), 0.0
    )
    prob_grads = jnp.einsum(
        "hwqd,hwkd->hwqk", grad_rows, value_rows, preferred_element_type=jnp.float32
    )
    score_grads = (prob_weights * (prob_grads - delta_part[..., None]) * score_scale).astype(
        jnp.bfloat16
    )
    return (prob_weights.astype(jnp.bfloat16), score_grads)


def pair_terms(probs_low, score_grads, query_rows, grad_rows):
    key_part = jnp.einsum(
        "hwqk,hwqd->hwkd", score_grads, query_rows, preferred_element_type=jnp.float32
    )
    value_part = jnp.einsum(
        "hwqk,hwqd->hwkd", probs_low, grad_rows, preferred_element_type=jnp.float32
    )
    return jnp.stack([key_part, value_part])


def body(queries, keys, values, grad_out, attn_out, window_mask):
    head_size = queries.shape[-1]
    score_scale = head_size ** (-0.5)
    tiles_wide = queries.shape[3]
    video_time = lax.axis_size("tm")
    video_height = lax.axis_size("height")
    time_local = lax.axis_index("tm") % video_time
    height_local = lax.axis_index("height") % video_height
    query_here = queries[0, 0]
    grads_here = grad_out[0, 0]
    output_here = attn_out[0, 0]
    mask_here = window_mask[0, 0]
    stacked_kv = jnp.stack([keys, values], axis=2)
    kv_block = with_halo(stacked_kv, (("tm", 0), ("height", 1)), 1)

    def inside(step_time, step_height):
        time_at = time_local + step_time - 1
        height_at = height_local + step_height - 1
        return (
            (time_at >= 0) & (time_at < video_time) & (height_at >= 0) & (height_at < video_height)
        )

    def width_span(step_width):
        return (max(0, 1 - step_width), min(tiles_wide, tiles_wide + 1 - step_width))

    def allowed_tiles(mask_rows, step_time, step_height, window_slot):
        picked = mask_rows != 0
        if window_slot == 13:
            picked = jnp.ones_like(picked)
        return picked & inside(step_time, step_height)

    offsets = [
        (step_time, step_height, step_width)
        for step_time in range(3)
        for step_height in range(3)
        for step_width in range(3)
        if width_span(step_width)[0] < width_span(step_width)[1]
    ]
    rows_shape = query_here.shape[:-1]
    running_top = jnp.full(rows_shape, -1e30, jnp.float32)
    running_total = jnp.zeros(rows_shape, jnp.float32)
    for step_time, step_height, step_width in offsets:
        start_at, stop_at = width_span(step_width)
        window_slot = 9 * step_time + 3 * step_height + step_width
        allowed = allowed_tiles(
            mask_here[start_at:stop_at, window_slot], step_time, step_height, window_slot
        )
        key_rows = kv_block[step_time, step_height, 0]

        def update(carried):
            top_all, total_all = carried
            scores = jnp.where(
                allowed[None, :, None, None], tile_scores(query_here, key_rows, score_scale), -1e30
            )
            new_top = jnp.maximum(top_all, scores.max(-1))
            new_total = total_all * jnp.exp(top_all - new_top) + jnp.exp(
                scores - new_top[..., None]
            ).sum(-1)
            return (
                top_all.at[:, start_at:stop_at].set(new_top),
                total_all.at[:, start_at:stop_at].set(new_total),
            )

        running_top, running_total = lax.cond(
            jnp.any(allowed), update, lambda carried: carried, (running_top, running_total)
        )
    log_total = running_top + jnp.log(running_total)
    delta_rows = jnp.sum(grads_here.astype(jnp.float32) * output_here.astype(jnp.float32), axis=-1)
    row_grads = jnp.zeros(query_here.shape, jnp.float32)
    columns = []
    for local_step_time in range(3):
        column_line = []
        for step_height in range(3):
            column = jnp.zeros((2,) + query_here.shape, jnp.float32)
            for step_width in range(3):
                local_start_at, local_stop_at = width_span(step_width)
                if local_start_at >= local_stop_at:
                    continue
                window_slot = 9 * local_step_time + 3 * step_height + step_width
                local_allowed = allowed_tiles(
                    mask_here[local_start_at:local_stop_at, window_slot],
                    local_step_time,
                    step_height,
                    window_slot,
                )
                kv_rows = kv_block[local_step_time, step_height]
                pair_count = local_stop_at - local_start_at
                row_shape = (query_here.shape[0], pair_count) + query_here.shape[2:]

                def active(unused):
                    probs_low, score_grads = probs_and_grads(
                        query_here,
                        grads_here,
                        log_total,
                        delta_rows,
                        kv_rows[0],
                        kv_rows[1],
                        local_allowed,
                        score_scale,
                    )
                    row_part = jnp.einsum(
                        "hwqk,hwkd->hwqd",
                        score_grads,
                        kv_rows[0],
                        preferred_element_type=jnp.float32,
                    )
                    return (row_part, pair_terms(probs_low, score_grads, query_here, grads_here))

                def silent(unused):
                    return (
                        jnp.zeros(row_shape, jnp.float32),
                        jnp.zeros((2,) + row_shape, jnp.float32),
                    )

                result = lax.cond(jnp.any(local_allowed), active, silent, 0)
                row_part, key_part = result
                column = column.at[
                    :, :, local_start_at + step_width - 1 : local_stop_at + step_width - 1
                ].add(key_part)
                row_grads = row_grads.at[:, local_start_at:local_stop_at].add(row_part)
            column_line.append(column.astype(jnp.bfloat16))
        columns.append(column_line)
    row_grads, columns = (row_grads, columns)
    columns = lax.optimization_barrier(columns)
    through_height = [columns[step_time][1].astype(jnp.float32) for step_time in range(3)]
    for shift_by, picked_side in ((1, 2), (-1, 0)):
        arrived = from_behind(
            jnp.stack([columns[step_time][picked_side] for step_time in range(3)]),
            "height",
            shift_by,
        )
        through_height = [
            through_height[step_time] + arrived[step_time].astype(jnp.float32)
            for step_time in range(3)
        ]
    key_grads = through_height[1]
    for shift_by, picked_side in ((1, 2), (-1, 0)):
        key_grads = key_grads + from_behind(
            through_height[picked_side].astype(jnp.bfloat16), "tm", shift_by
        ).astype(jnp.float32)
    grad_queries = row_grads.astype(jnp.bfloat16)[None, None]
    grad_keys = key_grads[0].astype(jnp.bfloat16)[None, None]
    grad_values = key_grads[1].astype(jnp.bfloat16)[None, None]
    return (grad_queries, grad_keys, grad_values)


def solution(mesh):
    placed = (
        P("tm", "height", "dp", None, None, None),
        P("tm", "height", "dp", None, None, None),
        P("tm", "height", "dp", None, None, None),
        P("tm", "height", "dp", None, None, None),
        P("tm", "height", "dp", None, None, None),
        P("tm", "height", None, None),
    )
    return jax.shard_map(
        body,
        mesh=mesh,
        in_specs=placed,
        out_specs=(
            P("tm", "height", "dp", None, None, None),
            P("tm", "height", "dp", None, None, None),
            P("tm", "height", "dp", None, None, None),
        ),
        check_vma=False,
    )
```

profile of v0, /device:TPU:1, one launch (start us, length us, event | category | flops | bytes accessed | tf_op | source)
XLA Modules:
  0.0 89.1 jit_solution(2902967711042058950)
XLA Ops:
  0.7 1.0 %pad_maximum_fusion.12 = bf16[1,1,2,2,1,192,128]{6,5,3,4,2,1,0:T(8,128)(2,1)S(1)} fusion(bf16[1,1,1,2,1,192,128]{6,5,3,4,2,1,0:T(8,128)(2,1)} %bitcast.547, bf16[1,1,1,2,1,192,128]{6,5,3,4,2,1,0:T(8,128)(2,1)} %bitcast.539), kind=kLoop, calls=%fused_computation.312 | loop fusion | flops 98304 | bytes 393216 | tf_op jit(solution)/shard_map/stack | solution.py:71
  1.7 4.6 %collective-permute-start = (bf16[1,1,2,2,1,192,128]{6,5,3,4,2,1,0:T(8,128)(2,1)S(1)}, bf16[1,1,2,2,1,192,128]{6,5,3,4,2,1,0:T(8,128)(2,1)S(1)}, u32[]{:S(2)}, u32[]{:S(2)}) collective-permute-start(bf16[1,1,2,2,1,192,128]{6,5,3,4,2,1,0:T(8,128)(2,1)S(1)} %pad_maximum_fusion.12), channel_id=1, source_target_pairs={{0,128},{128,256},{256,384},{384,512},{512,640},{640,768},{768,896... | collective-permute-start | bytes 589832 | tf_op jit(solution)/shard_map/ppermute | solution.py:14
  6.3 12.8 %collective-permute-start.1 = (bf16[1,1,2,2,1,192,128]{6,5,3,4,2,1,0:T(8,128)(2,1)S(1)}, bf16[1,1,2,2,1,192,128]{6,5,3,4,2,1,0:T(8,128)(2,1)S(1)}, u32[]{:S(2)}, u32[]{:S(2)}) collective-permute-start(bf16[1,1,2,2,1,192,128]{6,5,3,4,2,1,0:T(8,128)(2,1)S(1)} %pad_maximum_fusion.12), channel_id=1, source_target_pairs={{128,0},{256,128},{384,256},{512,384},{640,512},{768,640},{896,768... | collective-permute-start | bytes 589832 | tf_op jit(solution)/shard_map/ppermute | solution.py:15
  19.1 1.0 %collective-permute-done.1 = bf16[1,1,2,2,1,192,128]{6,5,3,4,2,1,0:T(8,128)(2,1)S(1)} collective-permute-done((bf16[1,1,2,2,1,192,128]{6,5,3,4,2,1,0:T(8,128)(2,1)S(1)}, bf16[1,1,2,2,1,192,128]{6,5,3,4,2,1,0:T(8,128)(2,1)S(1)}, u32[]{:S(2)}, u32[]{:S(2)}) %collective-permute-start.1) | collective-permute-done | bytes 196640 | tf_op jit(solution)/shard_map/ppermute | solution.py:15
  20.2 1.3 %collective-permute-start.2 = (bf16[3,1,2,2,1,192,128]{6,5,3,4,2,1,0:T(8,128)(2,1)S(1)}, bf16[3,1,2,2,1,192,128]{6,5,3,4,2,1,0:T(8,128)(2,1)S(1)}, u32[]{:S(2)}, u32[]{:S(2)}) collective-permute-start(bf16[3,1,2,2,1,192,128]{6,5,3,4,2,1,0:T(8,128)(2,1)S(1)} %pad_maximum_fusion.9), channel_id=1, source_target_pairs={{0,8},{8,16},{16,24},{24,32},{32,40},{40,48},{48,56},{56,64},{64,7... | collective-permute-start | bytes 1769480 | tf_op jit(solution)/shard_map/ppermute | solution.py:14
  27.4 1.3 %collective-permute-start.3 = (bf16[3,1,2,2,1,192,128]{6,5,3,4,2,1,0:T(8,128)(2,1)S(1)}, bf16[3,1,2,2,1,192,128]{6,5,3,4,2,1,0:T(8,128)(2,1)S(1)}, u32[]{:S(2)}, u32[]{:S(2)}) collective-permute-start(bf16[3,1,2,2,1,192,128]{6,5,3,4,2,1,0:T(8,128)(2,1)S(1)} %pad_maximum_fusion.9), channel_id=1, source_target_pairs={{8,0},{16,8},{24,16},{32,24},{40,32},{48,40},{56,48},{64,56},{72,6... | collective-permute-start | bytes 1769480 | tf_op jit(solution)/shard_map/ppermute | solution.py:15
  28.7 5.4 %collective-permute-done.2 = bf16[3,1,2,2,1,192,128]{6,5,3,4,2,1,0:T(8,128)(2,1)S(1)} collective-permute-done((bf16[3,1,2,2,1,192,128]{6,5,3,4,2,1,0:T(8,128)(2,1)S(1)}, bf16[3,1,2,2,1,192,128]{6,5,3,4,2,1,0:T(8,128)(2,1)S(1)}, u32[]{:S(2)}, u32[]{:S(2)}) %collective-permute-start.2) | collective-permute-done | bytes 589856 | tf_op jit(solution)/shard_map/ppermute | solution.py:14
  34.2 9.6 %collective-permute-done.3 = bf16[3,1,2,2,1,192,128]{6,5,3,4,2,1,0:T(8,128)(2,1)S(1)} collective-permute-done((bf16[3,1,2,2,1,192,128]{6,5,3,4,2,1,0:T(8,128)(2,1)S(1)}, bf16[3,1,2,2,1,192,128]{6,5,3,4,2,1,0:T(8,128)(2,1)S(1)}, u32[]{:S(2)}, u32[]{:S(2)}) %collective-permute-start.3) | collective-permute-done | bytes 589856 | tf_op jit(solution)/shard_map/ppermute | solution.py:15
  44.7 0.7 copy-done.3
  46.6 0.7 copy-done.11
  47.2 1.2 %conditional.31 = (f32[2,1,192,128]{3,2,0,1:T(8,128)S(1)}, bf16[2,2,1,192,128]{4,3,1,2,0:T(8,128)(2,1)S(1)}) conditional(s32[]{:T(128)} %convert_element_type.373, () %tuple.471, (pred[]{:T(512)}, bf16[2,1,192,128]{3,2,0,1:T(8,128)(2,1)S(1)}, bf16[1,1,2,2,1,192,128]{6,5,3,4,2,1,0:T(8,128)(2,1)S(1)}, f32[2,1,192]{2,0,1:T(2,128)S(1)}, ...), branch_computations={%region_45.46_spmd, %region_46.47_spmd} | conditional | flops 95158272 | bytes 2953233 | solution.py:173
  48.5 0.7 copy-done.5
  49.1 0.7 conditional.35
  49.2 0.7 broadcast.1729
  49.9 1.0 %pad_maximum_fusion.10 = bf16[3,2,2,1,192,128]{5,4,2,1,3,0:T(8,128)(2,1)S(1)} fusion(bf16[1,2,2,1,192,128]{5,4,2,1,3,0:T(8,128)(2,1)} %bitcast.185, bf16[1,2,2,1,192,128]{5,4,2,1,3,0:T(8,128)(2,1)S(1)} %bitcast.545, bf16[1,2,2,1,192,128]{5,4,2,1,3,0:T(8,128)(2,1)S(1)} %bitcast.543), kind=kLoop, calls=%fused_computation.291 | loop fusion | flops 589824 | bytes 1179648 | tf_op jit(solution)/shard_map/stack | solution.py:186
  50.9 1.3 %collective-permute-start.4 = (bf16[3,2,2,1,192,128]{5,4,2,1,3,0:T(8,128)(2,1)S(1)}, bf16[3,2,2,1,192,128]{5,4,2,1,3,0:T(8,128)(2,1)S(1)}, u32[]{:S(2)}, u32[]{:S(2)}) collective-permute-start(bf16[3,2,2,1,192,128]{5,4,2,1,3,0:T(8,128)(2,1)S(1)} %pad_maximum_fusion.10), channel_id=1, source_target_pairs={{0,8},{8,16},{16,24},{24,32},{32,40},{40,48},{48,56},{56,64},{64,7... | collective-permute-start | bytes 1769480 | tf_op jit(solution)/shard_map/ppermute | solution.py:23
  52.4 1.4 %collective-permute-start.5 = (bf16[3,2,2,1,192,128]{5,4,2,1,3,0:T(8,128)(2,1)S(1)}, bf16[3,2,2,1,192,128]{5,4,2,1,3,0:T(8,128)(2,1)S(1)}, u32[]{:S(2)}, u32[]{:S(2)}) collective-permute-start(bf16[3,2,2,1,192,128]{5,4,2,1,3,0:T(8,128)(2,1)S(1)} %pad_maximum_fusion.11), channel_id=1, source_target_pairs={{8,0},{16,8},{24,16},{32,24},{40,32},{48,40},{56,48},{64,56},{72,6... | collective-permute-start | bytes 1769480 | tf_op jit(solution)/shard_map/ppermute | solution.py:23
  53.8 6.8 %collective-permute-done.4 = bf16[3,2,2,1,192,128]{5,4,2,1,3,0:T(8,128)(2,1)S(1)} collective-permute-done((bf16[3,2,2,1,192,128]{5,4,2,1,3,0:T(8,128)(2,1)S(1)}, bf16[3,2,2,1,192,128]{5,4,2,1,3,0:T(8,128)(2,1)S(1)}, u32[]{:S(2)}, u32[]{:S(2)}) %collective-permute-start.4) | collective-permute-done | bytes 589856 | tf_op jit(solution)/shard_map/ppermute | solution.py:23
  60.6 10.1 %collective-permute-done.5 = bf16[3,2,2,1,192,128]{5,4,2,1,3,0:T(8,128)(2,1)S(1)} collective-permute-done((bf16[3,2,2,1,192,128]{5,4,2,1,3,0:T(8,128)(2,1)S(1)}, bf16[3,2,2,1,192,128]{5,4,2,1,3,0:T(8,128)(2,1)S(1)}, u32[]{:S(2)}, u32[]{:S(2)}) %collective-permute-start.5) | collective-permute-done | bytes 589856 | tf_op jit(solution)/shard_map/ppermute | solution.py:23
  70.8 10.4 %collective-permute-start.6 = (bf16[2,2,1,192,128]{4,3,1,0,2:T(8,128)(2,1)S(1)}, bf16[2,2,1,192,128]{4,3,1,0,2:T(8,128)(2,1)S(1)}, u32[]{:S(2)}, u32[]{:S(2)}) collective-permute-start(bf16[2,2,1,192,128]{4,3,1,0,2:T(8,128)(2,1)S(1)} %fusion.202), channel_id=1, source_target_pairs={{0,128},{128,256},{256,384},{384,512},{512,640},{640,768},{768,896... | collective-permute-start | bytes 589832 | tf_op jit(solution)/shard_map/ppermute | solution.py:23
  81.3 1.9 %collective-permute-start.7 = (bf16[2,2,1,192,128]{4,3,1,2,0:T(8,128)(2,1)S(1)}, bf16[2,2,1,192,128]{4,3,1,2,0:T(8,128)(2,1)S(1)}, u32[]{:S(2)}, u32[]{:S(2)}) collective-permute-start(bf16[2,2,1,192,128]{4,3,1,2,0:T(8,128)(2,1)S(1)} %fusion.200), channel_id=1, source_target_pairs={{128,0},{256,128},{384,256},{512,384},{640,512},{768,640},{896,768... | collective-permute-start | bytes 589832 | tf_op jit(solution)/shard_map/ppermute | solution.py:23
  83.3 0.7 fusion.208
  84.0 4.3 %collective-permute-done.7 = bf16[2,2,1,192,128]{4,3,1,2,0:T(8,128)(2,1)S(1)} collective-permute-done((bf16[2,2,1,192,128]{4,3,1,2,0:T(8,128)(2,1)S(1)}, bf16[2,2,1,192,128]{4,3,1,2,0:T(8,128)(2,1)S(1)}, u32[]{:S(2)}, u32[]{:S(2)}) %collective-permute-start.7) | collective-permute-done | bytes 196640 | tf_op jit(solution)/shard_map/ppermute | solution.py:23
  88.5 0.7 slice_bitcast_fusion.6
  (87 shorter events, 5.2 us)
Async XLA Ops:
  0.6 19.5 %copy-start.2 = (bf16[1,1,2,1,192,128]{5,4,3,2,1,0:T(8,128)(2,1)S(1)}, bf16[1,1,2,1,192,128]{5,4,3,2,1,0:T(8,128)(2,1)}, u32[]{:S(2)}) copy-start(bf16[1,1,2,1,192,128]{5,4,3,2,1,0:T(8,128)(2,1)} %param.187) | copy-start | bytes 294916
  0.6 19.5 %copy-start.13 = (bf16[1,1,2,1,192,128]{5,4,3,2,1,0:T(8,128)(2,1)S(1)}, bf16[1,1,2,1,192,128]{5,4,3,2,1,0:T(8,128)(2,1)}, u32[]{:S(2)}) copy-start(bf16[1,1,2,1,192,128]{5,4,3,2,1,0:T(8,128)(2,1)} %param.188) | copy-start | bytes 294916
  1.7 17.4 %copy-start.7 = (bf16[1,1,2,2,1,192,128]{6,5,3,4,2,1,0:T(8,128)(2,1)}, bf16[1,1,2,2,1,192,128]{6,5,3,4,2,1,0:T(8,128)(2,1)S(1)}, u32[]{:S(2)}) copy-start(bf16[1,1,2,2,1,192,128]{6,5,3,4,2,1,0:T(8,128)(2,1)S(1)} %pad_maximum_fusion.12) | copy-start | bytes 589828
  1.7 17.4 %collective-permute-start = (bf16[1,1,2,2,1,192,128]{6,5,3,4,2,1,0:T(8,128)(2,1)S(1)}, bf16[1,1,2,2,1,192,128]{6,5,3,4,2,1,0:T(8,128)(2,1)S(1)}, u32[]{:S(2)}, u32[]{:S(2)}) collective-permute-start(bf16[1,1,2,2,1,192,128]{6,5,3,4,2,1,0:T(8,128)(2,1)S(1)} %pad_maximum_fusion.12), channel_id=1, source_target_pairs={{0,128},{128,256},{256,384},{384,512},{512,640},{640,768},{768,896... | collective-permute-start | bytes 589832 | tf_op jit(solution)/shard_map/ppermute | solution.py:14
  6.3 13.8 %collective-permute-start.1 = (bf16[1,1,2,2,1,192,128]{6,5,3,4,2,1,0:T(8,128)(2,1)S(1)}, bf16[1,1,2,2,1,192,128]{6,5,3,4,2,1,0:T(8,128)(2,1)S(1)}, u32[]{:S(2)}, u32[]{:S(2)}) collective-permute-start(bf16[1,1,2,2,1,192,128]{6,5,3,4,2,1,0:T(8,128)(2,1)S(1)} %pad_maximum_fusion.12), channel_id=1, source_target_pairs={{128,0},{256,128},{384,256},{512,384},{640,512},{768,640},{896,768... | collective-permute-start | bytes 589832 | tf_op jit(solution)/shard_map/ppermute | solution.py:15
  20.2 1.3 %copy-start.15 = (s32[1,1,1,27]{3,2,1,0:T(1,128)S(1)}, s32[1,1,1,27]{3,2,1,0:T(1,128)}, u32[]{:S(2)}) copy-start(s32[1,1,1,27]{3,2,1,0:T(1,128)} %param.191) | copy-start | bytes 328
  20.2 13.9 %collective-permute-start.2 = (bf16[3,1,2,2,1,192,128]{6,5,3,4,2,1,0:T(8,128)(2,1)S(1)}, bf16[3,1,2,2,1,192,128]{6,5,3,4,2,1,0:T(8,128)(2,1)S(1)}, u32[]{:S(2)}, u32[]{:S(2)}) collective-permute-start(bf16[3,1,2,2,1,192,128]{6,5,3,4,2,1,0:T(8,128)(2,1)S(1)} %pad_maximum_fusion.9), channel_id=1, source_target_pairs={{0,8},{8,16},{16,24},{24,32},{32,40},{40,48},{48,56},{56,64},{64,7... | collective-permute-start | bytes 1769480 | tf_op jit(solution)/shard_map/ppermute | solution.py:14
  22.2 5.0 %copy-start.14 = (bf16[1,1,2,1,192,128]{5,4,3,2,1,0:T(8,128)(2,1)S(1)}, bf16[1,1,2,1,192,128]{5,4,3,2,1,0:T(8,128)(2,1)}, u32[]{:S(2)}) copy-start(bf16[1,1,2,1,192,128]{5,4,3,2,1,0:T(8,128)(2,1)} %param.190) | copy-start | bytes 294916
  22.2 5.0 %copy-start = (bf16[1,1,2,1,192,128]{5,4,3,2,1,0:T(8,128)(2,1)S(1)}, bf16[1,1,2,1,192,128]{5,4,3,2,1,0:T(8,128)(2,1)}, u32[]{:S(2)}) copy-start(bf16[1,1,2,1,192,128]{5,4,3,2,1,0:T(8,128)(2,1)} %param.189) | copy-start | bytes 294916
  27.4 16.4 %collective-permute-start.3 = (bf16[3,1,2,2,1,192,128]{6,5,3,4,2,1,0:T(8,128)(2,1)S(1)}, bf16[3,1,2,2,1,192,128]{6,5,3,4,2,1,0:T(8,128)(2,1)S(1)}, u32[]{:S(2)}, u32[]{:S(2)}) collective-permute-start(bf16[3,1,2,2,1,192,128]{6,5,3,4,2,1,0:T(8,128)(2,1)S(1)} %pad_maximum_fusion.9), channel_id=1, source_target_pairs={{8,0},{16,8},{24,16},{32,24},{40,32},{48,40},{56,48},{64,56},{72,6... | collective-permute-start | bytes 1769480 | tf_op jit(solution)/shard_map/ppermute | solution.py:15
  28.7 5.4 %copy-start.1 = (bf16[1,1,2,1,192,128]{5,4,3,2,1,0:T(8,128)(2,1)S(1)}, bf16[1,1,2,1,192,128]{5,4,3,2,1,0:T(8,128)(2,1)}, u32[]{:S(2)}) copy-start(bf16[1,1,2,1,192,128]{5,4,3,2,1,0:T(8,128)(2,1)} %param.186) | copy-start | bytes 294916
  44.7 0.7 copy-start.3
  45.5 0.7 copy-start.9
  45.5 1.0 %copy-start.8 = (bf16[1,1,2,2,1,192,128]{6,5,3,4,2,1,0:T(8,128)(2,1)S(1)}, bf16[1,1,2,2,1,192,128]{6,5,3,4,2,1,0:T(8,128)(2,1)}, u32[]{:S(2)}) copy-start(bf16[1,1,2,2,1,192,128]{6,5,3,4,2,1,0:T(8,128)(2,1)} %copy-done.7) | copy-start | bytes 589828
  46.5 0.7 copy-start.11
  48.5 0.7 copy-start.5
  49.9 2.4 %copy-start.4 = (bf16[2,2,1,192,128]{4,3,1,2,0:T(8,128)(2,1)S(1)}, bf16[2,2,1,192,128]{4,3,1,2,0:T(8,128)(2,1)}, u32[]{:S(2)}) copy-start(bf16[2,2,1,192,128]{4,3,1,2,0:T(8,128)(2,1)} %copy-done.3) | copy-start | bytes 589828
  50.9 9.7 %collective-permute-start.4 = (bf16[3,2,2,1,192,128]{5,4,2,1,3,0:T(8,128)(2,1)S(1)}, bf16[3,2,2,1,192,128]{5,4,2,1,3,0:T(8,128)(2,1)S(1)}, u32[]{:S(2)}, u32[]{:S(2)}) collective-permute-start(bf16[3,2,2,1,192,128]{5,4,2,1,3,0:T(8,128)(2,1)S(1)} %pad_maximum_fusion.10), channel_id=1, source_target_pairs={{0,8},{8,16},{16,24},{24,32},{32,40},{40,48},{48,56},{56,64},{64,7... | collective-permute-start | bytes 1769480 | tf_op jit(solution)/shard_map/ppermute | solution.py:23
  52.3 18.5 %copy-start.12 = (bf16[2,2,1,192,128]{4,3,1,2,0:T(8,128)(2,1)S(1)}, bf16[2,2,1,192,128]{4,3,1,2,0:T(8,128)(2,1)}, u32[]{:S(2)}) copy-start(bf16[2,2,1,192,128]{4,3,1,2,0:T(8,128)(2,1)} %copy-done.11) | copy-start | bytes 589828
  52.3 28.9 %copy-start.10 = (bf16[2,2,1,192,128]{4,3,1,2,0:T(8,128)(2,1)S(1)}, bf16[2,2,1,192,128]{4,3,1,2,0:T(8,128)(2,1)}, u32[]{:S(2)}) copy-start(bf16[2,2,1,192,128]{4,3,1,2,0:T(8,128)(2,1)} %copy-done.9) | copy-start | bytes 589828
  52.4 18.4 %collective-permute-start.5 = (bf16[3,2,2,1,192,128]{5,4,2,1,3,0:T(8,128)(2,1)S(1)}, bf16[3,2,2,1,192,128]{5,4,2,1,3,0:T(8,128)(2,1)S(1)}, u32[]{:S(2)}, u32[]{:S(2)}) collective-permute-start(bf16[3,2,2,1,192,128]{5,4,2,1,3,0:T(8,128)(2,1)S(1)} %pad_maximum_fusion.11), channel_id=1, source_target_pairs={{8,0},{16,8},{24,16},{32,24},{40,32},{48,40},{56,48},{64,56},{72,6... | collective-permute-start | bytes 1769480 | tf_op jit(solution)/shard_map/ppermute | solution.py:23
  70.8 13.2 %collective-permute-start.6 = (bf16[2,2,1,192,128]{4,3,1,0,2:T(8,128)(2,1)S(1)}, bf16[2,2,1,192,128]{4,3,1,0,2:T(8,128)(2,1)S(1)}, u32[]{:S(2)}, u32[]{:S(2)}) collective-permute-start(bf16[2,2,1,192,128]{4,3,1,0,2:T(8,128)(2,1)S(1)} %fusion.202), channel_id=1, source_target_pairs={{0,128},{128,256},{256,384},{384,512},{512,640},{640,768},{768,896... | collective-permute-start | bytes 589832 | tf_op jit(solution)/shard_map/ppermute | solution.py:23
  81.3 7.0 %collective-permute-start.7 = (bf16[2,2,1,192,128]{4,3,1,2,0:T(8,128)(2,1)S(1)}, bf16[2,2,1,192,128]{4,3,1,2,0:T(8,128)(2,1)S(1)}, u32[]{:S(2)}, u32[]{:S(2)}) collective-permute-start(bf16[2,2,1,192,128]{4,3,1,2,0:T(8,128)(2,1)S(1)} %fusion.200), channel_id=1, source_target_pairs={{128,0},{256,128},{384,256},{512,384},{640,512},{768,640},{896,768... | collective-permute-start | bytes 589832 | tf_op jit(solution)/shard_map/ppermute | solution.py:23
  83.3 5.1 %copy-start.6 = (bf16[2,2,1,192,128]{4,3,1,2,0:T(8,128)(2,1)S(1)}, bf16[2,2,1,192,128]{4,3,1,2,0:T(8,128)(2,1)}, u32[]{:S(2)}) copy-start(bf16[2,2,1,192,128]{4,3,1,2,0:T(8,128)(2,1)} %copy-done.5) | copy-start | bytes 589828
where the time goes:
time: 89.6 us; the launch traced here: 89.1 us
  waiting for transfers between devices  37.3 us (42%)
  starting transfers between devices  35 us (39%)
  between operations  6.09 us (7%)
  local copies, waits for them, and re-layouts  5.47 us (6%)
  other arithmetic  3.47 us (4%)
  matrix products  1.43 us (2%)
    ppermute x4, waiting for transfers between devices, from_behind(): return lax.ppermute(block, axis, route)  21.3 us
    ppermute x4, starting transfers between devices, from_behind(): return lax.ppermute(block, axis, route)  15.1 us
    ppermute x2, starting transfers between devices, with_halo(): after = lax.ppermute(initial, axis, down)  14.1 us
    ppermute x2, waiting for transfers between devices, with_halo(): after = lax.ppermute(initial, axis, down)  10.6 us
    ppermute x2, starting transfers between devices, with_halo(): before = lax.ppermute(last, axis, up)  5.92 us
    ppermute x2, waiting for transfers between devices, with_halo(): before = lax.ppermute(last, axis, up)  5.4 us
    unnamed x32, local copies, waits for them, and re-layouts  3.05 us
  transfers between devices with their start and end apart: 8, of which 6 were waited for; matrix products, arithmetic and copies ran while one was open for 2% of the time, Pallas kernels for 0%

commit v1 on v0

v1 whole, which is shorter than its diff:
```python
import functools

import jax
import jax.numpy as jnp
from jax import lax
from jax.experimental import pallas as pl
from jax.experimental.pallas import tpu as pltpu
from jax.sharding import PartitionSpec as P

MESH = pl.DeviceIdType.MESH
F32 = jnp.float32
BF16 = jnp.bfloat16
LOG2E = 1.4426950408889634
FAR = 1e30

SLOTS = ((0, 0), (-1, 0), (1, 0), (0, -1), (0, 1), (-1, -1), (1, -1), (-1, 1), (1, 1))
AHEAD = ((1, 0), (0, 1), (-1, 1), (1, 1))
SLOT_OF = {offset: slot for slot, offset in enumerate(SLOTS)}
K, V, Q, G = range(4)


def nt(a, b):
    return lax.dot_general(a, b, (((1,), (1,)), ((), ())), preferred_element_type=F32)


def nn(a, b):
    return lax.dot_general(a, b, (((1,), (0,)), ((), ())), preferred_element_type=F32)


def kernel(
    sizes,
    mask_ref,
    q_ref,
    k_ref,
    v_ref,
    g_ref,
    o_ref,
    dq_ref,
    dk_ref,
    dv_ref,
    tiles,
    out_tile,
    stat_out,
    stat_in,
    bias,
    run_max,
    run_sum,
    delta_col,
    dq_acc,
    dk_acc,
    dv_acc,
    local_sem,
    send_sem,
    recv_sem,
    stat_send,
    stat_recv,
    ready,
):
    n_t, n_h = sizes
    heads, rows, depth = q_ref.shape
    scale = depth**-0.5
    score_scale = scale * LOG2E
    t = lax.axis_index("tm")
    h = lax.axis_index("height")
    d = lax.axis_index("dp")
    inwards = 1 - 2 * lax.rem(d, 2)
    along = {side: (t + side * inwards >= 0) & (t + side * inwards < n_t) for side in (-1, 1)}
    up_down = {-1: h > 0, 1: h < n_h - 1}

    def exists(side, dh):
        if side == 0:
            return up_down[dh]
        return along[side] if dh == 0 else along[side] & up_down[dh]

    def device(side, dh):
        return (t + side * inwards, h + dh, d)

    def if_there(side, dh):
        return pl.when(exists(side, dh))

    def opposite(offset):
        return (-offset[0], -offset[1])

    barrier = pltpu.get_barrier_semaphore()
    for offset in AHEAD:

        @if_there(*offset)
        def _():
            pl.semaphore_signal(barrier, inc=1, device_id=device(*offset), device_id_type=MESH)

    sources = {K: k_ref, V: v_ref, Q: q_ref, G: g_ref}
    locals_ = [
        pltpu.make_async_copy(sources[x], tiles.at[x, :, 0], local_sem.at[x]) for x in (K, V, Q, G)
    ]
    locals_.append(pltpu.make_async_copy(o_ref, out_tile, local_sem.at[4]))
    for copy in locals_:
        copy.start()

    def copy_of(x, from_slot, side, dh):
        own_side, own_dh = SLOTS[from_slot]
        lands = SLOT_OF[(own_side - side, own_dh - dh)]
        return pltpu.make_async_remote_copy(
            src_ref=sources[x] if from_slot == 0 else tiles.at[x, :, from_slot],
            dst_ref=tiles.at[x, :, lands],
            send_sem=send_sem.at[x, lands],
            recv_sem=recv_sem.at[x, lands],
            device_id=device(side, dh),
            device_id_type=MESH,
        )

    def send(x, side, dh):
        if_there(side, dh)(lambda: copy_of(x, 0, side, dh).start())

    def arrived(x, slot):
        @if_there(*SLOTS[slot])
        def _():
            pltpu.make_async_copy(
                tiles.at[x, :, slot], tiles.at[x, :, slot], recv_sem.at[x, slot]
            ).wait()

    def forward(x, slot):
        arrived(x, slot)
        _, dh = SLOTS[slot]
        for side in (-1, 1):
            if_there(side, dh)(lambda: copy_of(x, slot, side, 0).start())

    for slot, (side, dh) in enumerate(SLOTS):
        if slot == 0:
            bias[slot] = jnp.float32(0)
        else:
            chosen = mask_ref[9 * (side * inwards + 1) + 3 * (dh + 1) + 1] != 0
            bias[slot] = jnp.where(exists(side, dh) & chosen, jnp.float32(0), jnp.float32(-FAR))

    for slot in range(1, 9):

        @pl.when(jnp.logical_not(exists(*SLOTS[slot])))
        def _():
            stat_in[slot, :heads] = jnp.full((heads, rows), FAR, F32)
            stat_in[slot, heads:] = jnp.zeros((heads, rows), F32)

            def clear(x, carry):
                tiles[x, :, slot] = jnp.zeros((heads, rows, depth), BF16)
                return carry

            lax.fori_loop(0, 4, clear, 0)

    def one(there):
        return there.astype(jnp.int32)

    @pl.when(along[-1] | up_down[-1])
    def _():
        pl.semaphore_wait(
            barrier, one(along[-1]) + one(up_down[-1]) * (1 + one(along[-1]) + one(along[1]))
        )

    for number, offset in enumerate(AHEAD):
        behind = opposite(offset)

        @if_there(*behind)
        def _():
            pl.semaphore_signal(
                ready.at[number], inc=1, device_id=device(*behind), device_id_type=MESH
            )

    def await_ready(number):
        if_there(*AHEAD[number])(lambda: pl.semaphore_wait(ready.at[number], 1))

    for x in (K, V):
        send(x, 0, -1)
        send(x, -1, 0)

    for copy in locals_:
        copy.wait()

    for head in range(heads):
        product = tiles[G, head, 0].astype(F32) * out_tile[head].astype(F32)
        delta_col[head] = jnp.sum(product, axis=1, keepdims=True)

    def as_row(column):
        return jnp.broadcast_to(column, (rows, 128)).T[:1]

    def query_side(slot, count):
        keys = count * rows
        bias_row = jnp.full((1, keys), bias[slot], F32)
        if count == 2:
            lane = lax.broadcasted_iota(jnp.int32, (1, keys), 1)
            bias_row = jnp.where(lane < rows, bias_row, bias[slot + 1])
        for head in range(heads):
            key_rows = tiles[K, head, slot : slot + count].reshape(keys, depth)
            value_rows = tiles[V, head, slot : slot + count].reshape(keys, depth)
            scores = nt(tiles[Q, head, 0], key_rows) * score_scale + bias_row
            top = jnp.max(scores, axis=1, keepdims=True)
            if slot > 0:
                old_max = run_max[head]
                top = jnp.maximum(old_max, top)
                decay = jnp.exp2(old_max - top)
            probs = jnp.exp2(scores - top)
            total = jnp.sum(probs, axis=1, keepdims=True)
            prob_grads = nt(tiles[G, head, 0], value_rows)
            score_grads = (probs * (prob_grads - delta_col[head])).astype(BF16)
            grads = nn(score_grads, key_rows)
            run_max[head] = top
            if slot > 0:
                run_sum[head] = run_sum[head] * decay + total
                dq_acc[head] = dq_acc[head] * decay + grads
            else:
                run_sum[head] = total
                dq_acc[head] = grads

    def key_side(slot, count, stats):
        queries = count * rows
        for head in range(heads):
            query_rows = tiles[Q, head, slot : slot + count].reshape(queries, depth)
            grad_rows = tiles[G, head, slot : slot + count].reshape(queries, depth)
            log_row = [stats[slot + i, head : head + 1] for i in range(count)]
            delta_row = [stats[slot + i, heads + head : heads + head + 1] for i in range(count)]
            if count == 2:
                log_row, delta_row = jnp.concatenate(log_row, 1), jnp.concatenate(delta_row, 1)
            else:
                log_row, delta_row = log_row[0], delta_row[0]
            probs = jnp.exp2(nt(tiles[K, head, 0], query_rows) * score_scale - log_row)
            prob_grads = nt(tiles[V, head, 0], grad_rows)
            score_grads = (probs * (prob_grads - delta_row)).astype(BF16)
            value_part = nn(probs.astype(BF16), grad_rows)
            key_part = nn(score_grads, query_rows)
            if slot == 0:
                dv_acc[head] = value_part
                dk_acc[head] = key_part
            else:
                dv_acc[head] += value_part
                dk_acc[head] += key_part

    def arrived_pair(x, slot):
        arrived(x, slot)
        arrived(x, slot + 1)

    query_side(0, 1)
    await_ready(0)
    send(K, 1, 0)
    send(V, 1, 0)
    await_ready(1)
    send(K, 0, 1)
    send(V, 0, 1)
    for offset in ((0, -1), (-1, 0), (1, 0), (0, 1)):
        send(Q, *offset)
    forward(K, 3)
    forward(K, 4)
    arrived_pair(K, 1)
    arrived_pair(V, 1)
    query_side(1, 2)
    forward(V, 3)
    forward(V, 4)
    for offset in ((0, -1), (-1, 0), (1, 0), (0, 1)):
        send(G, *offset)
    query_side(3, 2)
    forward(Q, 3)
    forward(Q, 4)
    arrived_pair(K, 5)
    arrived_pair(V, 5)
    query_side(5, 2)
    forward(G, 3)
    forward(G, 4)
    arrived_pair(K, 7)
    arrived_pair(V, 7)
    query_side(7, 2)

    for head in range(heads):
        log_total = as_row(run_max[head] + jnp.log2(run_sum[head]))
        delta = as_row(delta_col[head])
        for slot in range(9):
            stat_out[slot, head : head + 1] = log_total - bias[slot]
            stat_out[slot, heads + head : heads + head + 1] = delta

    def stat_copy(slot):
        lands = SLOT_OF[opposite(SLOTS[slot])]
        return pltpu.make_async_remote_copy(
            src_ref=stat_out.at[slot],
            dst_ref=stat_in.at[lands],
            send_sem=stat_send.at[slot],
            recv_sem=stat_recv.at[lands],
            device_id=device(*SLOTS[slot]),
            device_id_type=MESH,
        )

    await_ready(2)
    await_ready(3)
    for slot in range(1, 9):
        if_there(*SLOTS[slot])(lambda: stat_copy(slot).start())

    for head in range(heads):
        dq_ref[head] = (dq_acc[head] * (scale / run_sum[head])).astype(BF16)

    key_side(0, 1, stat_out)

    def stat_arrived(slot):
        @if_there(*SLOTS[slot])
        def _():
            pltpu.make_async_copy(stat_in.at[slot], stat_in.at[slot], stat_recv.at[slot]).wait()

    for slot in (1, 3, 5, 7):
        stat_arrived(slot)
        stat_arrived(slot + 1)
        if slot != 3:
            arrived_pair(Q, slot)
            arrived_pair(G, slot)
        key_side(slot, 2, stat_in)

    for head in range(heads):
        dk_ref[head] = (dk_acc[head] * scale).astype(BF16)
        dv_ref[head] = dv_acc[head].astype(BF16)

    for slot in range(1, 9):
        if_there(*SLOTS[slot])(lambda: stat_copy(slot).wait_send())
    for x in (K, V, Q, G):
        for offset in ((0, -1), (0, 1), (-1, 0), (1, 0)):
            if_there(*offset)(lambda: copy_of(x, 0, *offset).wait_send())
        for slot in (3, 4):
            for side in (-1, 1):
                if_there(side, SLOTS[slot][1])(lambda: copy_of(x, slot, side, 0).wait_send())


def body(sizes, queries, keys, values, grad_out, attn_out, window_mask):
    shape = queries.shape
    tile = (shape[2],) + shape[4:]
    heads, rows, depth = tile
    flat = [x.reshape(tile) for x in (queries, keys, values, grad_out, attn_out)]
    in_place = pl.BlockSpec(memory_space=pl.ANY)
    in_vmem = pl.BlockSpec(memory_space=pltpu.VMEM)
    outs = pl.pallas_call(
        functools.partial(kernel, sizes),
        out_shape=[jax.ShapeDtypeStruct(tile, BF16)] * 3,
        in_specs=[pl.BlockSpec(memory_space=pltpu.SMEM)] + [in_place] * 5,
        out_specs=[in_vmem] * 3,
        scratch_shapes=[
            pltpu.VMEM((4, heads, 9, rows, depth), BF16),
            pltpu.VMEM(tile, BF16),
            pltpu.VMEM((9, 2 * heads, rows), F32),
            pltpu.VMEM((9, 2 * heads, rows), F32),
            pltpu.SMEM((9,), F32),
            pltpu.VMEM((heads, rows, 1), F32),
            pltpu.VMEM((heads, rows, 1), F32),
            pltpu.VMEM((heads, rows, 1), F32),
            pltpu.VMEM(tile, F32),
            pltpu.VMEM(tile, F32),
            pltpu.VMEM(tile, F32),
            pltpu.SemaphoreType.DMA((5,)),
            pltpu.SemaphoreType.DMA((4, 9)),
            pltpu.SemaphoreType.DMA((4, 9)),
            pltpu.SemaphoreType.DMA((9,)),
            pltpu.SemaphoreType.DMA((9,)),
            pltpu.SemaphoreType.REGULAR((len(AHEAD),)),
        ],
        compiler_params=pltpu.CompilerParams(
            collective_id=0, has_side_effects=True, vmem_limit_bytes=54 << 20
        ),
        name="tile_attention_backward",
    )(window_mask.reshape(window_mask.shape[-1]), *flat)
    return tuple(x.reshape(shape) for x in outs)


def solution(mesh):
    sizes = (mesh.shape["tm"], mesh.shape["height"])
    tiled = P("tm", "height", "dp", None, None, None)
    return jax.shard_map(
        functools.partial(body, sizes),
        mesh=mesh,
        in_specs=(tiled,) * 5 + (P("tm", "height", None, None),),
        out_specs=(tiled,) * 3,
        check_vma=False,
    )
```

time: 89.6 us -> 38.4 us (0.43)
  waiting for transfers between devices: 37.3 us -> 0 us
  starting transfers between devices: 35 us -> 0 us
  Pallas kernels: 0 us -> 34.4 us
  between operations: 6.09 us -> 0.65 us
  other arithmetic: 3.47 us -> 0 us
  local copies, waits for them, and re-layouts: 5.47 us -> 3.15 us
  matrix products: 1.43 us -> 0 us
    ppermute x8 -> x0, waiting for transfers between devices: 37.3 us -> none  [the longest x4 21.3 us: from_behind(): return lax.ppermute(block, axis, route)]
    ppermute x8 -> x0, starting transfers between devices: 35 us -> none  [the longest x4 15.1 us: from_behind(): return lax.ppermute(block, axis, route)]
    pallas_call x0 -> x1, Pallas kernels: none -> 34.4 us  [body(): pl.pallas_call(functools.partial(kernel, sizes), out_shape=[jax.ShapeDtyp...]
    another operation x5 -> x0, other arithmetic: 2.25 us -> none  [the longest x2 1.1 us: body(): jnp.stack([columns[step_time][picked_side] for step_time in range(3)])]
    dot_general x6 -> x0, matrix products: 1.43 us -> none  [the longest x2 0.49 us: tile_scores(): jnp.einsum('hwqd,hwkd->hwqk', query_rows, key_rows, preferred_element_typ...]
    another operation x16 -> x0, local copies, waits for them, and re-layouts: 1.02 us -> none
    unnamed x32 -> x7, local copies, waits for them, and re-layouts: 3.05 us -> 3.15 us
  transfers between devices with their start and end apart: 8 -> 0, of which waited for: 6 -> 0; matrix products, arithmetic and copies ran while one was open for 2% -> 0% of each run, Pallas kernels for 0% -> 0%
where the time goes in v1:
time: 38.4 us; the launch traced here: 38.2 us
  Pallas kernels  34.4 us (90%)
  local copies, waits for them, and re-layouts  3.15 us (8%)
  between operations  0.65 us (2%)
    pallas_call x1, Pallas kernels, body(): pl.pallas_call(functools.partial(kernel, sizes), out_shape=[jax.ShapeDtyp...  34.4 us
    unnamed x7, local copies, waits for them, and re-layouts  3.15 us

profile of v1, /device:TPU:1, one launch (start us, length us, event | category | flops | bytes accessed | tf_op | source)
XLA Modules:
  0.0 38.2 jit_solution(15478461431016195351)
XLA Ops:
  0.6 34.4 %tile_attention_backward.1 = (bf16[2,192,128]{2,1,0:T(8,128)(2,1)}, bf16[2,192,128]{2,1,0:T(8,128)(2,1)}, bf16[2,192,128]{2,1,0:T(8,128)(2,1)}) custom-call(s32[27]{0:T(128)} %bitcast.23, bf16[2,192,128]{2,1,0:T(8,128)(2,1)} %bitcast.18, bf16[2,192,128]{2,1,0:T(8,128)(2,1)} %bitcast.19, bf16[2,192,128]{2,1,0:T(8,128)(2,1)} %bitcast.20, ...), custom_call_target="tpu_custom_call" | custom-call | tf_op jit(solution)/shard_map/tile_attention_backward/pallas_call | solution.py:329
  35.0 0.0 copy-start.1
  35.0 1.6 %copy.15 = bf16[1,1,2,1,192,128]{5,4,3,2,1,0:T(8,128)(2,1)} copy(bf16[1,1,2,1,192,128]{5,4,3,2,1,0:T(8,128)(2,1)} %bitcast.17) | data formatting | bytes 196608
  36.6 0.0 copy-done.1
  36.6 0.0 copy-start
  36.6 0.6 %copy.16 = bf16[1,1,2,1,192,128]{5,4,3,2,1,0:T(8,128)(2,1)} copy(bf16[1,1,2,1,192,128]{5,4,3,2,1,0:T(8,128)(2,1)S(1)} %bitcast.16) | data formatting | bytes 196608
  37.3 0.3 copy-done
  37.6 0.6 %copy.17 = bf16[1,1,2,1,192,128]{5,4,3,2,1,0:T(8,128)(2,1)} copy(bf16[1,1,2,1,192,128]{5,4,3,2,1,0:T(8,128)(2,1)S(1)} %bitcast.15) | data formatting | bytes 196608
Async XLA Ops:
  35.0 1.6 %copy-start.1 = (bf16[2,192,128]{2,1,0:T(8,128)(2,1)S(1)}, bf16[2,192,128]{2,1,0:T(8,128)(2,1)}, u32[]{:S(2)}) copy-start(bf16[2,192,128]{2,1,0:T(8,128)(2,1)} %get-tuple-element.7) | copy-start | bytes 294916
  36.6 0.9 %copy-start = (bf16[2,192,128]{2,1,0:T(8,128)(2,1)S(1)}, bf16[2,192,128]{2,1,0:T(8,128)(2,1)}, u32[]{:S(2)}) copy-start(bf16[2,192,128]{2,1,0:T(8,128)(2,1)} %get-tuple-element.8) | copy-start | bytes 294916

commit v2 on v1

--- a/solution.py
+++ b/solution.py
@@ -13,7 +13,7 @@
 LOG2E = 1.4426950408889634
 FAR = 1e30
 
-SLOTS = ((0, 0), (-1, 0), (1, 0), (0, -1), (0, 1), (-1, -1), (1, -1), (-1, 1), (1, 1))
+SLOTS = ((0, 0), (-1, 0), (1, 0), (0, -1), (0, 1), (-1, 1), (1, 1), (-1, -1), (1, -1))
 AHEAD = ((1, 0), (0, 1), (-1, 1), (1, 1))
 SLOT_OF = {offset: slot for slot, offset in enumerate(SLOTS)}
 K, V, Q, G = range(4)
@@ -63,8 +63,7 @@
     t = lax.axis_index("tm")
     h = lax.axis_index("height")
     d = lax.axis_index("dp")
-    inwards = 1 - 2 * lax.rem(d, 2)
-    along = {side: (t + side * inwards >= 0) & (t + side * inwards < n_t) for side in (-1, 1)}
+    along = {-1: t > 0, 1: t < n_t - 1}
     up_down = {-1: h > 0, 1: h < n_h - 1}
 
     def exists(side, dh):
@@ -72,8 +71,13 @@
             return up_down[dh]
         return along[side] if dh == 0 else along[side] & up_down[dh]
 
+    def origin(side, dh):
+        return (t + side == 0) & (h + dh == 0) & (d == 0)
+
+    direct = (t == 0) & (h == 1) & (d == 0)
+
     def device(side, dh):
-        return (t + side * inwards, h + dh, d)
+        return (t + side, h + dh, d)
 
     def if_there(side, dh):
         return pl.when(exists(side, dh))
@@ -82,11 +86,19 @@
         return (-offset[0], -offset[1])
 
     barrier = pltpu.get_barrier_semaphore()
+    at_origin = origin(0, 0)
+    by_origin = {offset: origin(*offset) for offset in ((-1, 0), (0, -1), (-1, -1))}
+    near_origin = by_origin[(-1, 0)] | by_origin[(0, -1)] | by_origin[(-1, -1)]
+
+    def signal(semaphore, offset, there):
+        @pl.when(there)
+        def _():
+            pl.semaphore_signal(semaphore, inc=1, device_id=device(*offset), device_id_type=MESH)
+
     for offset in AHEAD:
-
-        @if_there(*offset)
-        def _():
-            pl.semaphore_signal(barrier, inc=1, device_id=device(*offset), device_id_type=MESH)
+        signal(barrier, offset, exists(*offset) & jnp.logical_not(at_origin))
+    for offset, there in by_origin.items():
+        signal(barrier, offset, there)
 
     sources = {K: k_ref, V: v_ref, Q: q_ref, G: g_ref}
     locals_ = [
@@ -108,27 +120,51 @@
             device_id_type=MESH,
         )
 
-    def send(x, side, dh):
-        if_there(side, dh)(lambda: copy_of(x, 0, side, dh).start())
-
-    def arrived(x, slot):
-        @if_there(*SLOTS[slot])
+    def direct_copy(x):
+        slot = SLOT_OF[(-1, 1)]
+        return pltpu.make_async_remote_copy(
+            src_ref=sources[x],
+            dst_ref=tiles.at[x, :, slot],
+            send_sem=send_sem.at[x, 0],
+            recv_sem=recv_sem.at[x, slot],
+            device_id=device(1, -1),
+            device_id_type=MESH,
+        )
+
+    def in_turn(there, at_origin, late):
+        return there & (at_origin if late else jnp.logical_not(at_origin))
+
+    def send(x, side, dh, late=False):
+        there = exists(side, dh)
+        if (side, dh) in ((-1, 0), (0, -1)):
+            there = in_turn(there, origin(side, dh), late)
+        pl.when(there)(lambda: copy_of(x, 0, side, dh).start())
+
+    def arrived(x, slot, there=None):
+        @pl.when(exists(*SLOTS[slot]) if there is None else there)
         def _():
             pltpu.make_async_copy(
                 tiles.at[x, :, slot], tiles.at[x, :, slot], recv_sem.at[x, slot]
             ).wait()
 
-    def forward(x, slot):
-        arrived(x, slot)
-        _, dh = SLOTS[slot]
+    def pass_on(x, slot, side, there):
+        pl.when(there)(lambda: copy_of(x, slot, side, 0).start())
+
+    def forward_upper(x):
+        arrived(x, 4)
+        pass_on(x, 4, -1, in_turn(exists(-1, 1), origin(-1, 0), False))
+        pass_on(x, 4, 1, in_turn(exists(1, 1), origin(0, 0), False))
+
+    def forward_lower(x, late=False):
+        arrived(x, 3, in_turn(exists(0, -1), origin(0, -1), late))
         for side in (-1, 1):
-            if_there(side, dh)(lambda: copy_of(x, slot, side, 0).start())
+            pass_on(x, 3, side, in_turn(exists(side, -1), origin(0, -1), late))
 
     for slot, (side, dh) in enumerate(SLOTS):
         if slot == 0:
             bias[slot] = jnp.float32(0)
         else:
-            chosen = mask_ref[9 * (side * inwards + 1) + 3 * (dh + 1) + 1] != 0
+            chosen = mask_ref[9 * (side + 1) + 3 * (dh + 1) + 1] != 0
             bias[slot] = jnp.where(exists(side, dh) & chosen, jnp.float32(0), jnp.float32(-FAR))
 
     for slot in range(1, 9):
@@ -147,27 +183,33 @@
     def one(there):
         return there.astype(jnp.int32)
 
-    @pl.when(along[-1] | up_down[-1])
+    behind = one(along[-1]) + one(up_down[-1]) * (1 + one(along[-1]) + one(along[1]))
+    expected = behind - one(near_origin) + 3 * one(at_origin)
+
+    @pl.when(expected > 0)
     def _():
-        pl.semaphore_wait(
-            barrier, one(along[-1]) + one(up_down[-1]) * (1 + one(along[-1]) + one(along[1]))
-        )
+        pl.semaphore_wait(barrier, expected)
 
     for number, offset in enumerate(AHEAD):
-        behind = opposite(offset)
-
-        @if_there(*behind)
-        def _():
-            pl.semaphore_signal(
-                ready.at[number], inc=1, device_id=device(*behind), device_id_type=MESH
-            )
-
-    def await_ready(number):
-        if_there(*AHEAD[number])(lambda: pl.semaphore_wait(ready.at[number], 1))
+        there = exists(*opposite(offset))
+        if opposite(offset) in by_origin:
+            there = there & jnp.logical_not(by_origin[opposite(offset)])
+        signal(ready.at[number], opposite(offset), there)
+        if offset != (-1, 1):
+            signal(ready.at[len(AHEAD)], offset, at_origin)
+
+    def await_ready(number, there):
+        pl.when(there)(lambda: pl.semaphore_wait(ready.at[number], 1))
+
+    def await_ahead(number):
+        await_ready(number, exists(*AHEAD[number]) & jnp.logical_not(at_origin))
 
     for x in (K, V):
         send(x, 0, -1)
         send(x, -1, 0)
+        pl.when(direct)(lambda: direct_copy(x).start())
+        for offset in ((1, 0), (0, 1)):
+            pl.when(at_origin)(lambda: copy_of(x, 0, *offset).start())
 
     for copy in locals_:
         copy.wait()
@@ -181,16 +223,17 @@
 
     def query_side(slot, count):
         keys = count * rows
-        bias_row = jnp.full((1, keys), bias[slot], F32)
         if count == 2:
             lane = lax.broadcasted_iota(jnp.int32, (1, keys), 1)
-            bias_row = jnp.where(lane < rows, bias_row, bias[slot + 1])
+            bias_row = jnp.where(lane < rows, bias[slot], bias[slot + 1])
+        else:
+            bias_row = bias[slot]
         for head in range(heads):
-            key_rows = tiles[K, head, slot : slot + count].reshape(keys, depth)
-            value_rows = tiles[V, head, slot : slot + count].reshape(keys, depth)
+            key_rows = tiles[K, head, pl.ds(slot, count)].reshape(keys, depth)
+            value_rows = tiles[V, head, pl.ds(slot, count)].reshape(keys, depth)
             scores = nt(tiles[Q, head, 0], key_rows) * score_scale + bias_row
             top = jnp.max(scores, axis=1, keepdims=True)
-            if slot > 0:
+            if count == 2:
                 old_max = run_max[head]
                 top = jnp.maximum(old_max, top)
                 decay = jnp.exp2(old_max - top)
@@ -200,7 +243,7 @@
             score_grads = (probs * (prob_grads - delta_col[head])).astype(BF16)
             grads = nn(score_grads, key_rows)
             run_max[head] = top
-            if slot > 0:
+            if count == 2:
                 run_sum[head] = run_sum[head] * decay + total
                 dq_acc[head] = dq_acc[head] * decay + grads
             else:
@@ -234,35 +277,60 @@
         arrived(x, slot)
         arrived(x, slot + 1)
 
+    shift = one(origin(-1, 0)) + 2 * one(origin(0, -1))
+
+    def query_step(number):
+        step = lax.rem(number + shift, 4)
+        for at, slot in ((0, 1), (2, 5), (3, 7)):
+
+            @pl.when(step == at)
+            def _():
+                arrived_pair(K, slot)
+                arrived_pair(V, slot)
+
+        query_side(1 + 2 * step, 2)
+
     query_side(0, 1)
-    await_ready(0)
-    send(K, 1, 0)
-    send(V, 1, 0)
-    await_ready(1)
-    send(K, 0, 1)
-    send(V, 0, 1)
-    for offset in ((0, -1), (-1, 0), (1, 0), (0, 1)):
-        send(Q, *offset)
-    forward(K, 3)
-    forward(K, 4)
-    arrived_pair(K, 1)
-    arrived_pair(V, 1)
-    query_side(1, 2)
-    forward(V, 3)
-    forward(V, 4)
-    for offset in ((0, -1), (-1, 0), (1, 0), (0, 1)):
-        send(G, *offset)
-    query_side(3, 2)
-    forward(Q, 3)
-    forward(Q, 4)
-    arrived_pair(K, 5)
-    arrived_pair(V, 5)
-    query_side(5, 2)
-    forward(G, 3)
-    forward(G, 4)
-    arrived_pair(K, 7)
-    arrived_pair(V, 7)
-    query_side(7, 2)
+    await_ahead(0)
+    for x in (K, V):
+        pl.when(exists(1, 0) & jnp.logical_not(at_origin))(lambda: copy_of(x, 0, 1, 0).start())
+    await_ahead(1)
+    for x in (K, V):
+        pl.when(exists(0, 1) & jnp.logical_not(at_origin))(lambda: copy_of(x, 0, 0, 1).start())
+
+    def send_all(x):
+        send(x, 0, 1)
+        send(x, 1, 0)
+        send(x, 0, -1)
+        send(x, -1, 0)
+        pl.when(direct)(lambda: direct_copy(x).start())
+
+    send_all(Q)
+    forward_upper(K)
+    forward_lower(K)
+    forward_upper(V)
+    forward_lower(V)
+    query_step(0)
+    send_all(G)
+    query_step(1)
+    forward_upper(Q)
+    forward_lower(Q)
+    query_step(2)
+    forward_upper(G)
+    forward_lower(G)
+
+    await_ready(len(AHEAD), by_origin[(-1, 0)] | by_origin[(0, -1)])
+    for x in (K, V):
+        send(x, -1, 0, late=True)
+        send(x, 0, -1, late=True)
+        pass_on(x, 4, -1, in_turn(exists(-1, 1), origin(-1, 0), True))
+    for x in (K, V):
+        forward_lower(x, late=True)
+    for x in (Q, G):
+        send(x, -1, 0, late=True)
+        send(x, 0, -1, late=True)
+        pass_on(x, 4, -1, in_turn(exists(-1, 1), origin(-1, 0), True))
+    query_step(3)
 
     for head in range(heads):
         log_total = as_row(run_max[head] + jnp.log2(run_sum[head]))
@@ -282,10 +350,14 @@
             device_id_type=MESH,
         )
 
-    await_ready(2)
-    await_ready(3)
+    await_ahead(2)
+    await_ahead(3)
+    await_ready(len(AHEAD), by_origin[(-1, -1)])
     for slot in range(1, 9):
         if_there(*SLOTS[slot])(lambda: stat_copy(slot).start())
+
+    for x in (Q, G):
+        forward_lower(x, late=True)
 
     for head in range(heads):
         dq_ref[head] = (dq_acc[head] * (scale / run_sum[head])).astype(BF16)
@@ -314,9 +386,26 @@
     for x in (K, V, Q, G):
         for offset in ((0, -1), (0, 1), (-1, 0), (1, 0)):
             if_there(*offset)(lambda: copy_of(x, 0, *offset).wait_send())
-        for slot in (3, 4):
-            for side in (-1, 1):
-                if_there(side, SLOTS[slot][1])(lambda: copy_of(x, slot, side, 0).wait_send())
+        for side in (-1, 1):
+            if_there(side, -1)(lambda: copy_of(x, 3, side, 0).wait_send())
+        if_there(-1, 1)(lambda: copy_of(x, 4, -1, 0).wait_send())
+        pl.when(in_turn(exists(1, 1), origin(0, 0), False))(
+            lambda: copy_of(x, 4, 1, 0).wait_send()
+        )
+        pl.when(direct)(lambda: direct_copy(x).wait_send())
+
+
+def settle(*refs):
+    sources, targets, (semaphore, held) = refs[:3], refs[3:6], refs[6:]
+    loads = [pltpu.make_async_copy(sources[i], held.at[i], semaphore.at[i]) for i in range(3)]
+    stores = [pltpu.make_async_copy(held.at[i], targets[i], semaphore.at[3 + i]) for i in range(3)]
+    for load in loads:
+        load.start()
+    for load, store in zip(loads, stores):
+        load.wait()
+        store.start()
+    for store in stores:
+        store.wait()
 
 
 def body(sizes, queries, keys, values, grad_out, attn_out, window_mask):
@@ -348,13 +437,22 @@
             pltpu.SemaphoreType.DMA((4, 9)),
             pltpu.SemaphoreType.DMA((9,)),
             pltpu.SemaphoreType.DMA((9,)),
-            pltpu.SemaphoreType.REGULAR((len(AHEAD),)),
+            pltpu.SemaphoreType.REGULAR((len(AHEAD) + 1,)),
         ],
         compiler_params=pltpu.CompilerParams(
             collective_id=0, has_side_effects=True, vmem_limit_bytes=54 << 20
         ),
         name="tile_attention_backward",
     )(window_mask.reshape(window_mask.shape[-1]), *flat)
+    outs = pl.pallas_call(
+        settle,
+        out_shape=[jax.ShapeDtypeStruct(tile, BF16)] * 3,
+        in_specs=[in_place] * 3,
+        out_specs=[in_place] * 3,
+        scratch_shapes=[pltpu.SemaphoreType.DMA((6,)), pltpu.VMEM((3,) + tile, BF16)],
+        compiler_params=pltpu.CompilerParams(vmem_limit_bytes=54 << 20),
+        name="settle",
+    )(*outs)
     return tuple(x.reshape(shape) for x in outs)
 
 

time: 38.4 us -> 35.7 us (0.930)
  local copies, waits for them, and re-layouts: 3.15 us -> 0 us
  Pallas kernels: 34.4 us -> 34.8 us
    unnamed x7 -> x0, local copies, waits for them, and re-layouts: 3.15 us -> none
    pallas_call x0 -> x1, Pallas kernels: none -> 1.68 us  [body(): pl.pallas_call(settle, out_shape=[jax.ShapeDtypeStruct(tile, BF16)] * 3,...]
    pallas_call x1, Pallas kernels: 34.4 us -> 33.1 us  [body(): pl.pallas_call(functools.partial(kernel, sizes), out_shape=[jax.ShapeDtyp...]
where the time goes in v2:
time: 35.7 us; the launch traced here: 35.5 us
  Pallas kernels  34.8 us (97%)
  between operations  0.64 us (2%)
    pallas_call x1, Pallas kernels, body(): pl.pallas_call(functools.partial(kernel, sizes), out_shape=[jax.ShapeDtyp...  33.1 us
    pallas_call x1, Pallas kernels, body(): pl.pallas_call(settle, out_shape=[jax.ShapeDtypeStruct(tile, BF16)] * 3,...  1.68 us

profile of v2, /device:TPU:1, one launch (start us, length us, event | category | flops | bytes accessed | tf_op | source)
XLA Modules:
  0.0 35.5 jit_solution(2514180397232192788)
XLA Ops:
  0.6 33.1 %tile_attention_backward.1 = (bf16[2,192,128]{2,1,0:T(8,128)(2,1)}, bf16[2,192,128]{2,1,0:T(8,128)(2,1)}, bf16[2,192,128]{2,1,0:T(8,128)(2,1)}) custom-call(s32[27]{0:T(128)} %bitcast.20, bf16[2,192,128]{2,1,0:T(8,128)(2,1)} %bitcast.15, bf16[2,192,128]{2,1,0:T(8,128)(2,1)} %bitcast.16, bf16[2,192,128]{2,1,0:T(8,128)(2,1)} %bitcast.17, ...), custom_call_target="tpu_custom_call" | custom-call | tf_op jit(solution)/shard_map/tile_attention_backward/pallas_call | solution.py:418
  33.8 1.7 %settle.1 = (bf16[2,192,128]{2,1,0:T(8,128)(2,1)}, bf16[2,192,128]{2,1,0:T(8,128)(2,1)}, bf16[2,192,128]{2,1,0:T(8,128)(2,1)}) custom-call(bf16[2,192,128]{2,1,0:T(8,128)(2,1)} %get-tuple-element.9.refs_0_, bf16[2,192,128]{2,1,0:T(8,128)(2,1)} %get-tuple-element.10.refs_1_, bf16[2,192,128]{2,1,0:T(8,128)(2,1)} %get-tuple-element.11.refs_2_), custom_call_target="tpu_custom_call" | custom-call | tf_op jit(solution)/shard_map/settle/pallas_call | solution.py:447

commit v3 on v2

--- a/solution.py
+++ b/solution.py
@@ -38,6 +38,8 @@
     dq_ref,
     dk_ref,
     dv_ref,
+    mask,
+    results,
     tiles,
     out_tile,
     stat_out,
@@ -55,6 +57,8 @@
     stat_send,
     stat_recv,
     ready,
+    mask_sem,
+    out_sem,
 ):
     n_t, n_h = sizes
     heads, rows, depth = q_ref.shape
@@ -105,6 +109,8 @@
         pltpu.make_async_copy(sources[x], tiles.at[x, :, 0], local_sem.at[x]) for x in (K, V, Q, G)
     ]
     locals_.append(pltpu.make_async_copy(o_ref, out_tile, local_sem.at[4]))
+    mask_copy = pltpu.make_async_copy(mask_ref, mask, mask_sem)
+    mask_copy.start()
     for copy in locals_:
         copy.start()
 
@@ -160,26 +166,6 @@
         for side in (-1, 1):
             pass_on(x, 3, side, in_turn(exists(side, -1), origin(0, -1), late))
 
-    for slot, (side, dh) in enumerate(SLOTS):
-        if slot == 0:
-            bias[slot] = jnp.float32(0)
-        else:
-            chosen = mask_ref[9 * (side + 1) + 3 * (dh + 1) + 1] != 0
-            bias[slot] = jnp.where(exists(side, dh) & chosen, jnp.float32(0), jnp.float32(-FAR))
-
-    for slot in range(1, 9):
-
-        @pl.when(jnp.logical_not(exists(*SLOTS[slot])))
-        def _():
-            stat_in[slot, :heads] = jnp.full((heads, rows), FAR, F32)
-            stat_in[slot, heads:] = jnp.zeros((heads, rows), F32)
-
-            def clear(x, carry):
-                tiles[x, :, slot] = jnp.zeros((heads, rows, depth), BF16)
-                return carry
-
-            lax.fori_loop(0, 4, clear, 0)
-
     def one(there):
         return there.astype(jnp.int32)
 
@@ -210,6 +196,27 @@
         pl.when(direct)(lambda: direct_copy(x).start())
         for offset in ((1, 0), (0, 1)):
             pl.when(at_origin)(lambda: copy_of(x, 0, *offset).start())
+
+    mask_copy.wait()
+    for slot, (side, dh) in enumerate(SLOTS):
+        if slot == 0:
+            bias[slot] = jnp.float32(0)
+        else:
+            chosen = mask[0, 0, 0, 9 * (side + 1) + 3 * (dh + 1) + 1] != 0
+            bias[slot] = jnp.where(exists(side, dh) & chosen, jnp.float32(0), jnp.float32(-FAR))
+
+    for slot in range(1, 9):
+
+        @pl.when(jnp.logical_not(exists(*SLOTS[slot])))
+        def _():
+            stat_in[slot, :heads] = jnp.full((heads, rows), FAR, F32)
+            stat_in[slot, heads:] = jnp.zeros((heads, rows), F32)
+
+            def clear(x, carry):
+                tiles[x, :, slot] = jnp.zeros((heads, rows, depth), BF16)
+                return carry
+
+            lax.fori_loop(0, 4, clear, 0)
 
     for copy in locals_:
         copy.wait()
@@ -288,7 +295,8 @@
                 arrived_pair(K, slot)
                 arrived_pair(V, slot)
 
-        query_side(1 + 2 * step, 2)
+        empty = ((step == 2) & jnp.logical_not(up_down[1])) | ((step == 3) & jnp.logical_not(up_down[-1]))
+        pl.when(jnp.logical_not(empty))(lambda: query_side(1 + 2 * step, 2))
 
     query_side(0, 1)
     await_ahead(0)
@@ -360,7 +368,12 @@
         forward_lower(x, late=True)
 
     for head in range(heads):
-        dq_ref[head] = (dq_acc[head] * (scale / run_sum[head])).astype(BF16)
+        results[0, head] = (dq_acc[head] * (scale / run_sum[head])).astype(BF16)
+    out_copies = [
+        pltpu.make_async_copy(results.at[i], out, out_sem.at[i])
+        for i, out in enumerate((dq_ref, dk_ref, dv_ref))
+    ]
+    out_copies[0].start()
 
     key_side(0, 1, stat_out)
 
@@ -375,11 +388,17 @@
         if slot != 3:
             arrived_pair(Q, slot)
             arrived_pair(G, slot)
-        key_side(slot, 2, stat_in)
+        if slot < 5:
+            key_side(slot, 2, stat_in)
+        else:
+            pl.when(up_down[1 if slot == 5 else -1])(lambda: key_side(slot, 2, stat_in))
 
     for head in range(heads):
-        dk_ref[head] = (dk_acc[head] * scale).astype(BF16)
-        dv_ref[head] = dv_acc[head].astype(BF16)
+        results[1, head] = (dk_acc[head] * scale).astype(BF16)
+    out_copies[1].start()
+    for head in range(heads):
+        results[2, head] = dv_acc[head].astype(BF16)
+    out_copies[2].start()
 
     for slot in range(1, 9):
         if_there(*SLOTS[slot])(lambda: stat_copy(slot).wait_send())
@@ -393,6 +412,8 @@
             lambda: copy_of(x, 4, 1, 0).wait_send()
         )
         pl.when(direct)(lambda: direct_copy(x).wait_send())
+    for copy in out_copies:
+        copy.wait()
 
 
 def settle(*refs):
@@ -414,13 +435,14 @@
     heads, rows, depth = tile
     flat = [x.reshape(tile) for x in (queries, keys, values, grad_out, attn_out)]
     in_place = pl.BlockSpec(memory_space=pl.ANY)
-    in_vmem = pl.BlockSpec(memory_space=pltpu.VMEM)
     outs = pl.pallas_call(
         functools.partial(kernel, sizes),
         out_shape=[jax.ShapeDtypeStruct(tile, BF16)] * 3,
-        in_specs=[pl.BlockSpec(memory_space=pltpu.SMEM)] + [in_place] * 5,
-        out_specs=[in_vmem] * 3,
+        in_specs=[in_place] * 6,
+        out_specs=[in_place] * 3,
         scratch_shapes=[
+            pltpu.SMEM(window_mask.shape, jnp.int32),
+            pltpu.VMEM((3,) + tile, BF16),
             pltpu.VMEM((4, heads, 9, rows, depth), BF16),
             pltpu.VMEM(tile, BF16),
             pltpu.VMEM((9, 2 * heads, rows), F32),
@@ -438,12 +460,14 @@
             pltpu.SemaphoreType.DMA((9,)),
             pltpu.SemaphoreType.DMA((9,)),
             pltpu.SemaphoreType.REGULAR((len(AHEAD) + 1,)),
+            pltpu.SemaphoreType.DMA,
+            pltpu.SemaphoreType.DMA((3,)),
         ],
         compiler_params=pltpu.CompilerParams(
             collective_id=0, has_side_effects=True, vmem_limit_bytes=54 << 20
         ),
         name="tile_attention_backward",
-    )(window_mask.reshape(window_mask.shape[-1]), *flat)
+    )(window_mask, *flat)
     outs = pl.pallas_call(
         settle,
         out_shape=[jax.ShapeDtypeStruct(tile, BF16)] * 3,

time: 35.7 us -> 33.7 us (0.944)
  Pallas kernels: 34.8 us -> 32.9 us
    pallas_call x1, Pallas kernels: 33.1 us -> 31.2 us  [body(): pl.pallas_call(functools.partial(kernel, sizes), out_shape=[jax.ShapeDtyp...]
where the time goes in v3:
time: 33.7 us; the launch traced here: 33.5 us
  Pallas kernels  32.9 us (98%)
  between operations  0.64 us (2%)
    pallas_call x1, Pallas kernels, body(): pl.pallas_call(functools.partial(kernel, sizes), out_shape=[jax.ShapeDtyp...  31.2 us
    pallas_call x1, Pallas kernels, body(): pl.pallas_call(settle, out_shape=[jax.ShapeDtypeStruct(tile, BF16)] * 3,...  1.68 us

profile of v3, /device:TPU:1, one launch (start us, length us, event | category | flops | bytes accessed | tf_op | source)
XLA Modules:
  0.0 33.5 jit_solution(10075795726836976962)
XLA Ops:
  0.6 31.2 %tile_attention_backward.1 = (bf16[2,192,128]{2,1,0:T(8,128)(2,1)}, bf16[2,192,128]{2,1,0:T(8,128)(2,1)}, bf16[2,192,128]{2,1,0:T(8,128)(2,1)}) custom-call(s32[1,1,1,27]{3,2,1,0:T(1,128)} %mask_ref.1, bf16[2,192,128]{2,1,0:T(8,128)(2,1)} %bitcast.14, bf16[2,192,128]{2,1,0:T(8,128)(2,1)} %bitcast.15, bf16[2,192,128]{2,1,0:T(8,128)(2,1)} %bitcast.16, ...), custom_call_target="tpu_custom_call" | custom-call | tf_op jit(solution)/shard_map/tile_attention_backward/pallas_call | solution.py:438
  31.8 1.7 %settle.1 = (bf16[2,192,128]{2,1,0:T(8,128)(2,1)}, bf16[2,192,128]{2,1,0:T(8,128)(2,1)}, bf16[2,192,128]{2,1,0:T(8,128)(2,1)}) custom-call(bf16[2,192,128]{2,1,0:T(8,128)(2,1)} %get-tuple-element.9.refs_0_, bf16[2,192,128]{2,1,0:T(8,128)(2,1)} %get-tuple-element.10.refs_1_, bf16[2,192,128]{2,1,0:T(8,128)(2,1)} %get-tuple-element.11.refs_2_), custom_call_target="tpu_custom_call" | custom-call | tf_op jit(solution)/shard_map/settle/pallas_call | solution.py:471

commit v4 on v3

--- a/solution.py
+++ b/solution.py
@@ -157,7 +157,7 @@
         pl.when(there)(lambda: copy_of(x, slot, side, 0).start())
 
     def forward_upper(x):
-        arrived(x, 4)
+        arrived(x, 4, in_turn(exists(0, 1), at_origin, False))
         pass_on(x, 4, -1, in_turn(exists(-1, 1), origin(-1, 0), False))
         pass_on(x, 4, 1, in_turn(exists(1, 1), origin(0, 0), False))
 
@@ -260,8 +260,8 @@
     def key_side(slot, count, stats):
         queries = count * rows
         for head in range(heads):
-            query_rows = tiles[Q, head, slot : slot + count].reshape(queries, depth)
-            grad_rows = tiles[G, head, slot : slot + count].reshape(queries, depth)
+            query_rows = tiles[Q, head, pl.ds(slot, count)].reshape(queries, depth)
+            grad_rows = tiles[G, head, pl.ds(slot, count)].reshape(queries, depth)
             log_row = [stats[slot + i, head : head + 1] for i in range(count)]
             delta_row = [stats[slot + i, heads + head : heads + head + 1] for i in range(count)]
             if count == 2:
@@ -273,7 +273,7 @@
             score_grads = (probs * (prob_grads - delta_row)).astype(BF16)
             value_part = nn(probs.astype(BF16), grad_rows)
             key_part = nn(score_grads, query_rows)
-            if slot == 0:
+            if count == 1:
                 dv_acc[head] = value_part
                 dk_acc[head] = key_part
             else:
@@ -284,7 +284,11 @@
         arrived(x, slot)
         arrived(x, slot + 1)
 
-    shift = one(origin(-1, 0)) + 2 * one(origin(0, -1))
+    shift = one(origin(-1, 0)) + 2 * one(origin(0, -1)) + 2 * one(at_origin)
+
+    def is_empty(step):
+        upper = (step == 2) & jnp.logical_not(up_down[1])
+        return upper | ((step == 3) & jnp.logical_not(up_down[-1]))
 
     def query_step(number):
         step = lax.rem(number + shift, 4)
@@ -295,8 +299,7 @@
                 arrived_pair(K, slot)
                 arrived_pair(V, slot)
 
-        empty = ((step == 2) & jnp.logical_not(up_down[1])) | ((step == 3) & jnp.logical_not(up_down[-1]))
-        pl.when(jnp.logical_not(empty))(lambda: query_side(1 + 2 * step, 2))
+        pl.when(jnp.logical_not(is_empty(step)))(lambda: query_side(1 + 2 * step, 2))
 
     query_side(0, 1)
     await_ahead(0)
@@ -307,13 +310,22 @@
         pl.when(exists(0, 1) & jnp.logical_not(at_origin))(lambda: copy_of(x, 0, 0, 1).start())
 
     def send_all(x):
-        send(x, 0, 1)
-        send(x, 1, 0)
+        for offset in ((0, 1), (1, 0)):
+            there = exists(*offset)
+            if x == G:
+                there = in_turn(there, at_origin, False)
+            pl.when(there)(lambda: copy_of(x, 0, *offset).start())
         send(x, 0, -1)
         send(x, -1, 0)
         pl.when(direct)(lambda: direct_copy(x).start())
 
     send_all(Q)
+
+    @pl.when(at_origin)
+    def _():
+        copy_of(G, 0, 0, 1).start()
+        copy_of(G, 0, 1, 0).start()
+
     forward_upper(K)
     forward_lower(K)
     forward_upper(V)
@@ -334,6 +346,7 @@
         pass_on(x, 4, -1, in_turn(exists(-1, 1), origin(-1, 0), True))
     for x in (K, V):
         forward_lower(x, late=True)
+        arrived(x, 4, at_origin)
     for x in (Q, G):
         send(x, -1, 0, late=True)
         send(x, 0, -1, late=True)
@@ -366,6 +379,7 @@
 
     for x in (Q, G):
         forward_lower(x, late=True)
+        arrived(x, 4, at_origin)
 
     for head in range(heads):
         results[0, head] = (dq_acc[head] * (scale / run_sum[head])).astype(BF16)
@@ -382,16 +396,22 @@
         def _():
             pltpu.make_async_copy(stat_in.at[slot], stat_in.at[slot], stat_recv.at[slot]).wait()
 
-    for slot in (1, 3, 5, 7):
-        stat_arrived(slot)
-        stat_arrived(slot + 1)
-        if slot != 3:
-            arrived_pair(Q, slot)
-            arrived_pair(G, slot)
-        if slot < 5:
-            key_side(slot, 2, stat_in)
-        else:
-            pl.when(up_down[1 if slot == 5 else -1])(lambda: key_side(slot, 2, stat_in))
+    def key_step(number, carry):
+        step = lax.rem(number + shift, 4)
+        for at, slot in enumerate((1, 3, 5, 7)):
+
+            @pl.when(step == at)
+            def _():
+                stat_arrived(slot)
+                stat_arrived(slot + 1)
+                if slot != 3:
+                    arrived_pair(Q, slot)
+                    arrived_pair(G, slot)
+
+        pl.when(jnp.logical_not(is_empty(step)))(lambda: key_side(1 + 2 * step, 2, stat_in))
+        return carry
+
+    lax.fori_loop(0, 4, key_step, 0)
 
     for head in range(heads):
         results[1, head] = (dk_acc[head] * scale).astype(BF16)

time: 33.7 us -> 31 us (0.920)
  Pallas kernels: 32.9 us -> 30.1 us
    pallas_call x1, Pallas kernels: 31.2 us -> 28.5 us  [body(): pl.pallas_call(functools.partial(kernel, sizes), out_shape=[jax.ShapeDtyp...]
where the time goes in v4:
time: 31 us; the launch traced here: 30.8 us
  Pallas kernels  30.1 us (97%)
  between operations  0.64 us (2%)
    pallas_call x1, Pallas kernels, body(): pl.pallas_call(functools.partial(kernel, sizes), out_shape=[jax.ShapeDtyp...  28.5 us
    pallas_call x1, Pallas kernels, body(): pl.pallas_call(settle, out_shape=[jax.ShapeDtypeStruct(tile, BF16)] * 3,...  1.68 us

profile of v4, /device:TPU:1, one launch (start us, length us, event | category | flops | bytes accessed | tf_op | source)
XLA Modules:
  0.0 30.8 jit_solution(18219285222624640368)
XLA Ops:
  0.6 28.5 %tile_attention_backward.1 = (bf16[2,192,128]{2,1,0:T(8,128)(2,1)}, bf16[2,192,128]{2,1,0:T(8,128)(2,1)}, bf16[2,192,128]{2,1,0:T(8,128)(2,1)}) custom-call(s32[1,1,1,27]{3,2,1,0:T(1,128)} %mask_ref.1, bf16[2,192,128]{2,1,0:T(8,128)(2,1)} %bitcast.14, bf16[2,192,128]{2,1,0:T(8,128)(2,1)} %bitcast.15, bf16[2,192,128]{2,1,0:T(8,128)(2,1)} %bitcast.16, ...), custom_call_target="tpu_custom_call" | custom-call | tf_op jit(solution)/shard_map/tile_attention_backward/pallas_call | solution.py:458
  29.1 1.7 %settle.1 = (bf16[2,192,128]{2,1,0:T(8,128)(2,1)}, bf16[2,192,128]{2,1,0:T(8,128)(2,1)}, bf16[2,192,128]{2,1,0:T(8,128)(2,1)}) custom-call(bf16[2,192,128]{2,1,0:T(8,128)(2,1)} %get-tuple-element.9.refs_0_, bf16[2,192,128]{2,1,0:T(8,128)(2,1)} %get-tuple-element.10.refs_1_, bf16[2,192,128]{2,1,0:T(8,128)(2,1)} %get-tuple-element.11.refs_2_), custom_call_target="tpu_custom_call" | custom-call | tf_op jit(solution)/shard_map/settle/pallas_call | solution.py:491

commit v5 on v4

--- a/solution.py
+++ b/solution.py
@@ -14,7 +14,7 @@
 FAR = 1e30
 
 SLOTS = ((0, 0), (-1, 0), (1, 0), (0, -1), (0, 1), (-1, 1), (1, 1), (-1, -1), (1, -1))
-AHEAD = ((1, 0), (0, 1), (-1, 1), (1, 1))
+AHEAD = ((0, 1), (-1, 1), (1, 1))
 SLOT_OF = {offset: slot for slot, offset in enumerate(SLOTS)}
 K, V, Q, G = range(4)
 
@@ -45,6 +45,7 @@
     stat_out,
     stat_in,
     bias,
+    held_scores,
     run_max,
     run_sum,
     delta_col,
@@ -99,10 +100,10 @@
         def _():
             pl.semaphore_signal(semaphore, inc=1, device_id=device(*offset), device_id_type=MESH)
 
-    for offset in AHEAD:
+    for offset in AHEAD + ((-1, 0), (1, 0)):
         signal(barrier, offset, exists(*offset) & jnp.logical_not(at_origin))
-    for offset, there in by_origin.items():
-        signal(barrier, offset, there)
+    for offset in ((0, -1), (-1, -1)):
+        signal(barrier, offset, by_origin[offset])
 
     sources = {K: k_ref, V: v_ref, Q: q_ref, G: g_ref}
     locals_ = [
@@ -169,8 +170,8 @@
     def one(there):
         return there.astype(jnp.int32)
 
-    behind = one(along[-1]) + one(up_down[-1]) * (1 + one(along[-1]) + one(along[1]))
-    expected = behind - one(near_origin) + 3 * one(at_origin)
+    sides = one(along[-1]) + one(along[1])
+    expected = sides + one(up_down[-1]) * (1 + sides) - one(near_origin) + 2 * one(at_origin)
 
     @pl.when(expected > 0)
     def _():
@@ -181,8 +182,8 @@
         if opposite(offset) in by_origin:
             there = there & jnp.logical_not(by_origin[opposite(offset)])
         signal(ready.at[number], opposite(offset), there)
-        if offset != (-1, 1):
-            signal(ready.at[len(AHEAD)], offset, at_origin)
+    for offset in ((1, 0), (0, 1), (1, 1)):
+        signal(ready.at[len(AHEAD)], offset, at_origin)
 
     def await_ready(number, there):
         pl.when(there)(lambda: pl.semaphore_wait(ready.at[number], 1))
@@ -193,9 +194,9 @@
     for x in (K, V):
         send(x, 0, -1)
         send(x, -1, 0)
+        send(x, 1, 0)
         pl.when(direct)(lambda: direct_copy(x).start())
-        for offset in ((1, 0), (0, 1)):
-            pl.when(at_origin)(lambda: copy_of(x, 0, *offset).start())
+        pl.when(at_origin)(lambda: copy_of(x, 0, 0, 1).start())
 
     mask_copy.wait()
     for slot, (side, dh) in enumerate(SLOTS):
@@ -228,7 +229,7 @@
     def as_row(column):
         return jnp.broadcast_to(column, (rows, 128)).T[:1]
 
-    def query_side(slot, count):
+    def score_side(slot, count, index):
         keys = count * rows
         if count == 2:
             lane = lax.broadcasted_iota(jnp.int32, (1, keys), 1)
@@ -237,24 +238,30 @@
             bias_row = bias[slot]
         for head in range(heads):
             key_rows = tiles[K, head, pl.ds(slot, count)].reshape(keys, depth)
-            value_rows = tiles[V, head, pl.ds(slot, count)].reshape(keys, depth)
             scores = nt(tiles[Q, head, 0], key_rows) * score_scale + bias_row
+            held_scores[index, head, :, :keys] = scores
             top = jnp.max(scores, axis=1, keepdims=True)
             if count == 2:
                 old_max = run_max[head]
                 top = jnp.maximum(old_max, top)
-                decay = jnp.exp2(old_max - top)
-            probs = jnp.exp2(scores - top)
-            total = jnp.sum(probs, axis=1, keepdims=True)
+            total = jnp.sum(jnp.exp2(scores - top), axis=1, keepdims=True)
+            if count == 2:
+                total = run_sum[head] * jnp.exp2(old_max - top) + total
+            run_max[head] = top
+            run_sum[head] = total
+
+    def query_side(slot, count, index):
+        keys = count * rows
+        for head in range(heads):
+            key_rows = tiles[K, head, pl.ds(slot, count)].reshape(keys, depth)
+            value_rows = tiles[V, head, pl.ds(slot, count)].reshape(keys, depth)
+            probs = jnp.exp2(held_scores[index, head, :, :keys] - run_max[head])
             prob_grads = nt(tiles[G, head, 0], value_rows)
             score_grads = (probs * (prob_grads - delta_col[head])).astype(BF16)
             grads = nn(score_grads, key_rows)
-            run_max[head] = top
             if count == 2:
-                run_sum[head] = run_sum[head] * decay + total
-                dq_acc[head] = dq_acc[head] * decay + grads
+                dq_acc[head] += grads
             else:
-                run_sum[head] = total
                 dq_acc[head] = grads
 
     def key_side(slot, count, stats):
@@ -290,22 +297,20 @@
         upper = (step == 2) & jnp.logical_not(up_down[1])
         return upper | ((step == 3) & jnp.logical_not(up_down[-1]))
 
-    def query_step(number):
+    def step_of(x, side, number):
         step = lax.rem(number + shift, 4)
         for at, slot in ((0, 1), (2, 5), (3, 7)):
-
-            @pl.when(step == at)
-            def _():
-                arrived_pair(K, slot)
-                arrived_pair(V, slot)
-
-        pl.when(jnp.logical_not(is_empty(step)))(lambda: query_side(1 + 2 * step, 2))
-
-    query_side(0, 1)
+            pl.when(step == at)(lambda: arrived_pair(x, slot))
+        pl.when(jnp.logical_not(is_empty(step)))(lambda: side(1 + 2 * step, 2, 1 + step))
+
+    def score_step(number):
+        step_of(K, score_side, number)
+
+    def query_step(number):
+        step_of(V, query_side, number)
+
+    score_side(0, 1, 0)
     await_ahead(0)
-    for x in (K, V):
-        pl.when(exists(1, 0) & jnp.logical_not(at_origin))(lambda: copy_of(x, 0, 1, 0).start())
-    await_ahead(1)
     for x in (K, V):
         pl.when(exists(0, 1) & jnp.logical_not(at_origin))(lambda: copy_of(x, 0, 0, 1).start())
 
@@ -328,33 +333,26 @@
 
     forward_upper(K)
     forward_lower(K)
+    score_step(0)
+    score_step(1)
     forward_upper(V)
     forward_lower(V)
-    query_step(0)
     send_all(G)
-    query_step(1)
-    forward_upper(Q)
-    forward_lower(Q)
-    query_step(2)
-    forward_upper(G)
-    forward_lower(G)
+    score_step(2)
 
     await_ready(len(AHEAD), by_origin[(-1, 0)] | by_origin[(0, -1)])
     for x in (K, V):
         send(x, -1, 0, late=True)
         send(x, 0, -1, late=True)
         pass_on(x, 4, -1, in_turn(exists(-1, 1), origin(-1, 0), True))
-    for x in (K, V):
-        forward_lower(x, late=True)
-        arrived(x, 4, at_origin)
-    for x in (Q, G):
-        send(x, -1, 0, late=True)
-        send(x, 0, -1, late=True)
-        pass_on(x, 4, -1, in_turn(exists(-1, 1), origin(-1, 0), True))
-    query_step(3)
+    forward_lower(K, late=True)
+    arrived(K, 4, at_origin)
+    score_step(3)
 
     for head in range(heads):
-        log_total = as_row(run_max[head] + jnp.log2(run_sum[head]))
+        run_max[head] += jnp.log2(run_sum[head])
+    for head in range(heads):
+        log_total = as_row(run_max[head])
         delta = as_row(delta_col[head])
         for slot in range(9):
             stat_out[slot, head : head + 1] = log_total - bias[slot]
@@ -371,18 +369,33 @@
             device_id_type=MESH,
         )
 
+    await_ahead(1)
     await_ahead(2)
-    await_ahead(3)
     await_ready(len(AHEAD), by_origin[(-1, -1)])
     for slot in range(1, 9):
         if_there(*SLOTS[slot])(lambda: stat_copy(slot).start())
 
+    forward_lower(V, late=True)
+    arrived(V, 4, at_origin)
+    forward_upper(Q)
+    forward_lower(Q)
+    query_side(0, 1, 0)
+    query_step(0)
+    forward_upper(G)
+    forward_lower(G)
+    for x in (Q, G):
+        send(x, -1, 0, late=True)
+        send(x, 0, -1, late=True)
+        pass_on(x, 4, -1, in_turn(exists(-1, 1), origin(-1, 0), True))
+    query_step(1)
+    query_step(2)
+    query_step(3)
     for x in (Q, G):
         forward_lower(x, late=True)
         arrived(x, 4, at_origin)
 
     for head in range(heads):
-        results[0, head] = (dq_acc[head] * (scale / run_sum[head])).astype(BF16)
+        results[0, head] = (dq_acc[head] * scale).astype(BF16)
     out_copies = [
         pltpu.make_async_copy(results.at[i], out, out_sem.at[i])
         for i, out in enumerate((dq_ref, dk_ref, dv_ref))
@@ -468,6 +481,7 @@
             pltpu.VMEM((9, 2 * heads, rows), F32),
             pltpu.VMEM((9, 2 * heads, rows), F32),
             pltpu.SMEM((9,), F32),
+            pltpu.VMEM((5, heads, rows, 2 * rows), F32),
             pltpu.VMEM((heads, rows, 1), F32),
             pltpu.VMEM((heads, rows, 1), F32),
             pltpu.VMEM((heads, rows, 1), F32),

time: 31 us -> 28.7 us (0.926)
  Pallas kernels: 30.1 us -> 27.6 us
    pallas_call x1, Pallas kernels: 28.5 us -> 25.9 us  [body(): pl.pallas_call(functools.partial(kernel, sizes), out_shape=[jax.ShapeDtyp...]
where the time goes in v5:
time: 28.7 us; the launch traced here: 28.2 us
  Pallas kernels  27.6 us (96%)
  between operations  0.64 us (2%)
    pallas_call x1, Pallas kernels, body(): pl.pallas_call(functools.partial(kernel, sizes), out_shape=[jax.ShapeDtyp...  25.9 us
    pallas_call x1, Pallas kernels, body(): pl.pallas_call(settle, out_shape=[jax.ShapeDtypeStruct(tile, BF16)] * 3,...  1.68 us

profile of v5, /device:TPU:1, one launch (start us, length us, event | category | flops | bytes accessed | tf_op | source)
XLA Modules:
  0.0 28.2 jit_solution(1071045205238361366)
XLA Ops:
  0.6 25.9 %tile_attention_backward.1 = (bf16[2,192,128]{2,1,0:T(8,128)(2,1)}, bf16[2,192,128]{2,1,0:T(8,128)(2,1)}, bf16[2,192,128]{2,1,0:T(8,128)(2,1)}) custom-call(s32[1,1,1,27]{3,2,1,0:T(1,128)} %mask_ref.1, bf16[2,192,128]{2,1,0:T(8,128)(2,1)} %bitcast.14, bf16[2,192,128]{2,1,0:T(8,128)(2,1)} %bitcast.15, bf16[2,192,128]{2,1,0:T(8,128)(2,1)} %bitcast.16, ...), custom_call_target="tpu_custom_call" | custom-call | tf_op jit(solution)/shard_map/tile_attention_backward/pallas_call | solution.py:471
  26.5 1.7 %settle.1 = (bf16[2,192,128]{2,1,0:T(8,128)(2,1)}, bf16[2,192,128]{2,1,0:T(8,128)(2,1)}, bf16[2,192,128]{2,1,0:T(8,128)(2,1)}) custom-call(bf16[2,192,128]{2,1,0:T(8,128)(2,1)} %get-tuple-element.9.refs_0_, bf16[2,192,128]{2,1,0:T(8,128)(2,1)} %get-tuple-element.10.refs_1_, bf16[2,192,128]{2,1,0:T(8,128)(2,1)} %get-tuple-element.11.refs_2_), custom_call_target="tpu_custom_call" | custom-call | tf_op jit(solution)/shard_map/settle/pallas_call | solution.py:505

commit v6 on v5

--- a/solution.py
+++ b/solution.py
@@ -157,15 +157,15 @@
     def pass_on(x, slot, side, there):
         pl.when(there)(lambda: copy_of(x, slot, side, 0).start())
 
-    def forward_upper(x):
-        arrived(x, 4, in_turn(exists(0, 1), at_origin, False))
-        pass_on(x, 4, -1, in_turn(exists(-1, 1), origin(-1, 0), False))
-        pass_on(x, 4, 1, in_turn(exists(1, 1), origin(0, 0), False))
-
-    def forward_lower(x, late=False):
-        arrived(x, 3, in_turn(exists(0, -1), origin(0, -1), late))
+    def forward_upper(x, now=True):
+        arrived(x, 4, in_turn(exists(0, 1), at_origin, False) & now)
+        pass_on(x, 4, -1, in_turn(exists(-1, 1), origin(-1, 0), False) & now)
+        pass_on(x, 4, 1, in_turn(exists(1, 1), origin(0, 0), False) & now)
+
+    def forward_lower(x, late=False, now=True):
+        arrived(x, 3, in_turn(exists(0, -1), origin(0, -1), late) & now)
         for side in (-1, 1):
-            pass_on(x, 3, side, in_turn(exists(side, -1), origin(0, -1), late))
+            pass_on(x, 3, side, in_turn(exists(side, -1), origin(0, -1), late) & now)
 
     def one(there):
         return there.astype(jnp.int32)
@@ -191,12 +191,14 @@
     def await_ahead(number):
         await_ready(number, exists(*AHEAD[number]) & jnp.logical_not(at_origin))
 
-    for x in (K, V):
+    def send_first(x):
         send(x, 0, -1)
         send(x, -1, 0)
         send(x, 1, 0)
         pl.when(direct)(lambda: direct_copy(x).start())
         pl.when(at_origin)(lambda: copy_of(x, 0, 0, 1).start())
+
+    send_first(K)
 
     mask_copy.wait()
     for slot, (side, dh) in enumerate(SLOTS):
@@ -310,6 +312,7 @@
         step_of(V, query_side, number)
 
     score_side(0, 1, 0)
+    send_first(V)
     await_ahead(0)
     for x in (K, V):
         pl.when(exists(0, 1) & jnp.logical_not(at_origin))(lambda: copy_of(x, 0, 0, 1).start())
@@ -339,14 +342,21 @@
     forward_lower(V)
     send_all(G)
     score_step(2)
+    for x in (Q, G):
+        forward_upper(x, near_origin)
+        forward_lower(x, now=near_origin)
 
     await_ready(len(AHEAD), by_origin[(-1, 0)] | by_origin[(0, -1)])
-    for x in (K, V):
+
+    def send_late(x):
         send(x, -1, 0, late=True)
         send(x, 0, -1, late=True)
         pass_on(x, 4, -1, in_turn(exists(-1, 1), origin(-1, 0), True))
+
+    send_late(K)
     forward_lower(K, late=True)
     arrived(K, 4, at_origin)
+    send_late(V)
     score_step(3)
 
     for head in range(heads):
@@ -377,16 +387,14 @@
 
     forward_lower(V, late=True)
     arrived(V, 4, at_origin)
-    forward_upper(Q)
-    forward_lower(Q)
+    forward_upper(Q, jnp.logical_not(near_origin))
+    forward_lower(Q, now=jnp.logical_not(near_origin))
     query_side(0, 1, 0)
     query_step(0)
-    forward_upper(G)
-    forward_lower(G)
-    for x in (Q, G):
-        send(x, -1, 0, late=True)
-        send(x, 0, -1, late=True)
-        pass_on(x, 4, -1, in_turn(exists(-1, 1), origin(-1, 0), True))
+    forward_upper(G, jnp.logical_not(near_origin))
+    forward_lower(G, now=jnp.logical_not(near_origin))
+    send_late(Q)
+    send_late(G)
     query_step(1)
     query_step(2)
     query_step(3)
@@ -409,8 +417,10 @@
         def _():
             pltpu.make_async_copy(stat_in.at[slot], stat_in.at[slot], stat_recv.at[slot]).wait()
 
+    key_shift = shift + one(origin(-2, -1)) + 2 * one(origin(-1, -2))
+
     def key_step(number, carry):
-        step = lax.rem(number + shift, 4)
+        step = lax.rem(number + key_shift, 4)
         for at, slot in enumerate((1, 3, 5, 7)):
 
             @pl.when(step == at)

time: 28.7 us -> 28.7 us (level)
  no operation moved by 1% of the time
where the time goes in v6:
time: 28.7 us; the launch traced here: 28.3 us
  Pallas kernels  27.7 us (97%)
  between operations  0.64 us (2%)
    pallas_call x1, Pallas kernels, body(): pl.pallas_call(functools.partial(kernel, sizes), out_shape=[jax.ShapeDtyp...  26 us
    pallas_call x1, Pallas kernels, body(): pl.pallas_call(settle, out_shape=[jax.ShapeDtypeStruct(tile, BF16)] * 3,...  1.68 us

profile of v6, /device:TPU:1, one launch (start us, length us, event | category | flops | bytes accessed | tf_op | source)
XLA Modules:
  0.0 28.3 jit_solution(1334903637689778064)
XLA Ops:
  0.6 26.0 %tile_attention_backward.1 = (bf16[2,192,128]{2,1,0:T(8,128)(2,1)}, bf16[2,192,128]{2,1,0:T(8,128)(2,1)}, bf16[2,192,128]{2,1,0:T(8,128)(2,1)}) custom-call(s32[1,1,1,27]{3,2,1,0:T(1,128)} %mask_ref.1, bf16[2,192,128]{2,1,0:T(8,128)(2,1)} %bitcast.14, bf16[2,192,128]{2,1,0:T(8,128)(2,1)} %bitcast.15, bf16[2,192,128]{2,1,0:T(8,128)(2,1)} %bitcast.16, ...), custom_call_target="tpu_custom_call" | custom-call | tf_op jit(solution)/shard_map/tile_attention_backward/pallas_call | solution.py:481
  26.6 1.7 %settle.1 = (bf16[2,192,128]{2,1,0:T(8,128)(2,1)}, bf16[2,192,128]{2,1,0:T(8,128)(2,1)}, bf16[2,192,128]{2,1,0:T(8,128)(2,1)}) custom-call(bf16[2,192,128]{2,1,0:T(8,128)(2,1)} %get-tuple-element.9.refs_0_, bf16[2,192,128]{2,1,0:T(8,128)(2,1)} %get-tuple-element.10.refs_1_, bf16[2,192,128]{2,1,0:T(8,128)(2,1)} %get-tuple-element.11.refs_2_), custom_call_target="tpu_custom_call" | custom-call | tf_op jit(solution)/shard_map/settle/pallas_call | solution.py:515

commit v7 on v6

--- a/solution.py
+++ b/solution.py
@@ -191,14 +191,12 @@
     def await_ahead(number):
         await_ready(number, exists(*AHEAD[number]) & jnp.logical_not(at_origin))
 
-    def send_first(x):
+    for x in (K, V):
         send(x, 0, -1)
         send(x, -1, 0)
         send(x, 1, 0)
         pl.when(direct)(lambda: direct_copy(x).start())
         pl.when(at_origin)(lambda: copy_of(x, 0, 0, 1).start())
-
-    send_first(K)
 
     mask_copy.wait()
     for slot, (side, dh) in enumerate(SLOTS):
@@ -312,7 +310,6 @@
         step_of(V, query_side, number)
 
     score_side(0, 1, 0)
-    send_first(V)
     await_ahead(0)
     for x in (K, V):
         pl.when(exists(0, 1) & jnp.logical_not(at_origin))(lambda: copy_of(x, 0, 0, 1).start())
@@ -347,16 +344,12 @@
         forward_lower(x, now=near_origin)
 
     await_ready(len(AHEAD), by_origin[(-1, 0)] | by_origin[(0, -1)])
-
-    def send_late(x):
+    for x in (K, V):
         send(x, -1, 0, late=True)
         send(x, 0, -1, late=True)
         pass_on(x, 4, -1, in_turn(exists(-1, 1), origin(-1, 0), True))
-
-    send_late(K)
     forward_lower(K, late=True)
     arrived(K, 4, at_origin)
-    send_late(V)
     score_step(3)
 
     for head in range(heads):
@@ -393,8 +386,10 @@
     query_step(0)
     forward_upper(G, jnp.logical_not(near_origin))
     forward_lower(G, now=jnp.logical_not(near_origin))
-    send_late(Q)
-    send_late(G)
+    for x in (Q, G):
+        send(x, -1, 0, late=True)
+        send(x, 0, -1, late=True)
+        pass_on(x, 4, -1, in_turn(exists(-1, 1), origin(-1, 0), True))
     query_step(1)
     query_step(2)
     query_step(3)
@@ -417,10 +412,8 @@
         def _():
             pltpu.make_async_copy(stat_in.at[slot], stat_in.at[slot], stat_recv.at[slot]).wait()
 
-    key_shift = shift + one(origin(-2, -1)) + 2 * one(origin(-1, -2))
-
     def key_step(number, carry):
-        step = lax.rem(number + key_shift, 4)
+        step = lax.rem(number + shift, 4)
         for at, slot in enumerate((1, 3, 5, 7)):
 
             @pl.when(step == at)

time: 28.7 us -> 28.8 us (level)
  no operation moved by 1% of the time
where the time goes in v7:
time: 28.8 us; the launch traced here: 28.2 us
  Pallas kernels  27.6 us (96%)
  between operations  0.64 us (2%)
    pallas_call x1, Pallas kernels, body(): pl.pallas_call(functools.partial(kernel, sizes), out_shape=[jax.ShapeDtyp...  25.9 us
    pallas_call x1, Pallas kernels, body(): pl.pallas_call(settle, out_shape=[jax.ShapeDtypeStruct(tile, BF16)] * 3,...  1.68 us

profile of v7, /device:TPU:1, one launch (start us, length us, event | category | flops | bytes accessed | tf_op | source)
XLA Modules:
  0.0 28.2 jit_solution(635546369838750448)
XLA Ops:
  0.6 25.9 %tile_attention_backward.1 = (bf16[2,192,128]{2,1,0:T(8,128)(2,1)}, bf16[2,192,128]{2,1,0:T(8,128)(2,1)}, bf16[2,192,128]{2,1,0:T(8,128)(2,1)}) custom-call(s32[1,1,1,27]{3,2,1,0:T(1,128)} %mask_ref.1, bf16[2,192,128]{2,1,0:T(8,128)(2,1)} %bitcast.14, bf16[2,192,128]{2,1,0:T(8,128)(2,1)} %bitcast.15, bf16[2,192,128]{2,1,0:T(8,128)(2,1)} %bitcast.16, ...), custom_call_target="tpu_custom_call" | custom-call | tf_op jit(solution)/shard_map/tile_attention_backward/pallas_call | solution.py:474
  26.6 1.7 %settle.1 = (bf16[2,192,128]{2,1,0:T(8,128)(2,1)}, bf16[2,192,128]{2,1,0:T(8,128)(2,1)}, bf16[2,192,128]{2,1,0:T(8,128)(2,1)}) custom-call(bf16[2,192,128]{2,1,0:T(8,128)(2,1)} %get-tuple-element.9.refs_0_, bf16[2,192,128]{2,1,0:T(8,128)(2,1)} %get-tuple-element.10.refs_1_, bf16[2,192,128]{2,1,0:T(8,128)(2,1)} %get-tuple-element.11.refs_2_), custom_call_target="tpu_custom_call" | custom-call | tf_op jit(solution)/shard_map/settle/pallas_call | solution.py:508
